TPU v7x, 128 devices: a whole 4x4x4 slice. The times are simulated.
128 devices in a mesh: section: 8 (over x, core), tp: 16 (over z, y).
Axes of the slice: x: 4, y: 4, z: 4, core: 2. Of those that a mesh axis runs over, the one named last changes fastest.
Arguments:
- layer_inputs: bfloat16 [16, 512, 4096], P('section', None, 'tp'), may hold values from -6 to 6
- weights: bfloat16 [16, 4096, 4096], P('section', 'tp'), may hold values from -0.046875 to 0.046875
- input_basis: bfloat16 [16, 4096, 64], P('section', 'tp'), may hold values from -0.09375 to 0.09375
- output_basis: bfloat16 [16, 4096, 32], P('section', 'tp'), may hold values from -0.09375 to 0.09375
- queries: bfloat16 [16, 512, 2048], P('section', 'tp'), may hold values from -0.00390625 to 0.00390625
- top_cotangent: bfloat16 [512, 4096], replicated, may hold values from -6 to 6
- sequence_example: int32 [4], replicated, may hold values from 0 to 1
Outputs:
- scores: float32 [2, 512], P(None, 'tp')
All inputs are finite; a program needn't handle non-finite values.
Results may differ from a plain program's by a relative error of at most 0.0094.
Values may be sent and summed in bfloat16 or wider, within the bound.
No kernel may reach another device: no remote copies, remote signals or barrier semaphores. Data moves between devices by JAX's collectives and lax.ppermute only.
A program may use at most 64 MiB of HBM per device.

v0:
```python
import jax
import jax.numpy as jnp
from jax import lax
from jax.sharding import PartitionSpec as P

SEQLEN = 128
SEQ_MB = 1
MB = 4
EXAMPLES = 2


def from_behind(value, axis, by):
    size = lax.axis_size(axis)
    pairs = [(i, i + by) for i in range(size) if 0 <= i + by < size]
    return lax.ppermute(value, axis, pairs)


def silu_parts(values):
    floats = values.astype(jnp.float32)
    logistic = jax.nn.sigmoid(floats)
    return ((floats * logistic).astype(jnp.bfloat16), logistic * (1.0 + floats * (1.0 - logistic)))


def contract_columns(portion, matrix):
    return lax.dot_general(
        portion, matrix, (((1,), (1,)), ((), ())), preferred_element_type=jnp.float32
    )


def outer_rows(out_feats, in_feats):
    joined = out_feats[:, :, :, None] * in_feats[:, :, None, :]
    return joined.reshape(joined.shape[0], joined.shape[1], -1)


def shards(
    layer_inputs, weights, input_basis, output_basis, queries, top_cotangent, sequence_example
):
    section_count = lax.axis_size("section")
    section_rank = lax.axis_index("section")
    tp_rank = lax.axis_index("tp")
    width_local = layer_inputs.shape[2]
    width_full = weights.shape[2]
    total_tokens = layer_inputs.shape[1]
    block_rows = SEQ_MB * SEQLEN
    activated, slopes = silu_parts(layer_inputs)
    partial_in = jnp.einsum(
        "ltd,ldr->tlr", activated, input_basis, preferred_element_type=jnp.float32
    )
    in_feats = lax.psum(partial_in.reshape(total_tokens, -1), "tp").reshape(partial_in.shape)
    example_index = jnp.arange(EXAMPLES, dtype=jnp.int32)
    is_top = section_rank == section_count - 1

    def fold_lower(portion):
        return contract_columns(portion, weights[0])

    def tick(tick_index, state):
        outgoing, grads, stored = state
        micro_index = tick_index - (section_count - 1 - section_rank)
        valid = (micro_index >= 0) & (micro_index < MB)
        micro_clip = jnp.clip(micro_index, 0, MB - 1)
        first_row = micro_clip * block_rows
        slope_block = lax.dynamic_slice_in_dim(slopes, first_row, block_rows, 1)
        received = from_behind(outgoing, "section", -1)
        top_block = lax.dynamic_slice_in_dim(top_cotangent, first_row, block_rows, 0)
        upper_full = jnp.where(is_top, top_block, received)
        upper_own = lax.dynamic_slice_in_dim(upper_full, tp_rank * width_local, width_local, 1)
        upper_branch = lax.dot_general(
            upper_full, weights[1], (((1,), (1,)), ((), ())), preferred_element_type=jnp.float32
        )
        middle_own = (upper_own.astype(jnp.float32) + slope_block[1] * upper_branch).astype(
            jnp.bfloat16
        )
        lower_branch = fold_lower(lax.all_gather(middle_own, "tp", axis=1, tiled=True))
        lower_own = (middle_own.astype(jnp.float32) + slope_block[0] * lower_branch).astype(
            jnp.bfloat16
        )
        new_outgoing = lax.all_gather(lower_own, "tp", axis=1, tiled=True)
        cotangents = jnp.stack([middle_own, upper_own], 0)
        partial_out = jnp.einsum(
            "lrd,ldk->rlk", cotangents, output_basis, preferred_element_type=jnp.float32
        )
        out_feats = lax.psum(partial_out.reshape(block_rows, -1), "tp").reshape(partial_out.shape)
        in_block = lax.dynamic_slice_in_dim(in_feats, first_row, block_rows, 0)
        block_examples = jnp.repeat(
            lax.dynamic_slice_in_dim(sequence_example, micro_clip * SEQ_MB, SEQ_MB, 0), SEQLEN
        )
        selector = (example_index[:, None] == block_examples[None, :]).astype(
            jnp.float32
        ) * valid.astype(jnp.float32)
        grads = grads + jnp.einsum(
            "er,rlk->lek",
            selector,
            outer_rows(out_feats, in_block),
            precision=lax.Precision.HIGHEST,
        )
        return (new_outgoing, grads, stored)

    outgoing_init = jnp.zeros((block_rows, width_full), jnp.bfloat16)
    grads_init = jnp.zeros((2, EXAMPLES, queries.shape[2]), jnp.float32)
    stored_init = jnp.zeros((1,), jnp.bfloat16)
    final_out, grads, stored = lax.fori_loop(
        0, MB + section_count - 1, tick, (outgoing_init, grads_init, stored_init)
    )
    layer_scores = jnp.einsum(
        "lek,lqk->eq", grads, queries.astype(jnp.float32), precision=lax.Precision.HIGHEST
    )
    return lax.psum(layer_scores, "section")


def solution(mesh):
    placed = (
        P("section", None, "tp"),
        P("section", "tp", None),
        P("section", "tp", None),
        P("section", "tp", None),
        P("section", "tp", None),
        P(),
        P(),
    )
    return jax.shard_map(
        shards, mesh=mesh, in_specs=placed, out_specs=P(None, "tp"), check_vma=False
    )
```

profile of v0, /device:TPU:1, one launch (start us, length us, event | category | flops | bytes accessed | tf_op | source)
XLA Modules:
  0.0 1662.4 jit_solution(13824720775074881913)
XLA Ops:
  9.2 87.7 %all-reduce.2.cloned.1.call-done = f32[512,2,64]{0,2,1:T(8,128)} async-done(((f32[512,2,64]{0,2,1:T(8,128)}), f32[512,2,64]{0,2,1:T(8,128)}) %all-reduce.2.cloned.1.call-update) | async-done | bytes 262160 | tf_op jit(solution)/shard_map/psum | solution.py:49
  98.0 1529.4 %while.18 = (s32[]{:T(128)}, bf16[128,4096]{1,0:T(8,128)(2,1)}, f32[2,2,2048]{2,1,0:T(2,128)S(1)}, pred[]{:T(512)}, s32[]{:T(128)}, /*index=5*/bf16[512,4096]{1,...) while((s32[]{:T(128)}, bf16[128,4096]{1,0:T(8,128)(2,1)}, ...), condition=%wide.region_3.4_spmd.clone, body=%wide.region_1.3_spmd.clone.sunk | while | flops 555048960 | bytes 25986044 | solution.py:101
  98.0 3.9 collective-permute-start
  101.9 13.7 collective-permute-done
  120.3 40.6 %all-gather.3.cloned.1.call-done = bf16[128,4096]{1,0:T(8,128)(2,1)} async-done(((bf16[128,256]{1,0:T(8,128)(2,1)}), bf16[128,4096]{1,0:T(8,128)(2,1)}) %all-gather.3.cloned.1.call-update) | async-done | bytes 1048592 | tf_op jit(solution)/shard_map/while/body/eval_jaxpr/all_gather | solution.py:73
  160.9 3.3 add_convert_fusion.5
  166.6 58.4 %psum.31 = f32[128,2,32]{0,2,1:T(8,128)S(1)} all-reduce(f32[128,2,32]{0,2,1:T(8,128)S(1)} %convolution_bitcast_fusion.5), channel_id=1, replica_groups=mesh['section'=8,'tp'=16] {'tp'}, use_global_device_ids=true, to_apply=%region_2.2 | all-reduce | flops 8192 | bytes 65536 | tf_op jit(solution)/shard_map/while/body/eval_jaxpr/psum | solution.py:82
  227.2 17.7 %collective-permute-start = (bf16[128,4096]{1,0:T(8,128)(2,1)}, bf16[128,4096]{1,0:T(8,128)(2,1)S(1)}, u32[]{:S(2)}, u32[]{:S(2)}) collective-permute-start(bf16[128,4096]{1,0:T(8,128)(2,1)} %get-tuple-element.465), channel_id=1, source_target_pairs={{16,0},{32,16},{48,32},{64,48},{80,64},{96,80},{112,96},{17,1},{33... | collective-permute-start | bytes 3145736 | tf_op jit(solution)/shard_map/while/body/eval_jaxpr/ppermute | solution.py:15
  244.9 13.7 collective-permute-done
  263.3 37.6 %all-gather.3.cloned.1.call-done = bf16[128,4096]{1,0:T(8,128)(2,1)} async-done(((bf16[128,256]{1,0:T(8,128)(2,1)}), bf16[128,4096]{1,0:T(8,128)(2,1)}) %all-gather.3.cloned.1.call-update) | async-done | bytes 1048592 | tf_op jit(solution)/shard_map/while/body/eval_jaxpr/all_gather | solution.py:73
  306.6 58.4 %psum.31 = f32[128,2,32]{0,2,1:T(8,128)S(1)} all-reduce(f32[128,2,32]{0,2,1:T(8,128)S(1)} %convolution_bitcast_fusion.5), channel_id=1, replica_groups=mesh['section'=8,'tp'=16] {'tp'}, use_global_device_ids=true, to_apply=%region_2.2 | all-reduce | flops 8192 | bytes 65536 | tf_op jit(solution)/shard_map/while/body/eval_jaxpr/psum | solution.py:82
  367.3 17.7 %collective-permute-start = (bf16[128,4096]{1,0:T(8,128)(2,1)}, bf16[128,4096]{1,0:T(8,128)(2,1)S(1)}, u32[]{:S(2)}, u32[]{:S(2)}) collective-permute-start(bf16[128,4096]{1,0:T(8,128)(2,1)} %get-tuple-element.465), channel_id=1, source_target_pairs={{16,0},{32,16},{48,32},{64,48},{80,64},{96,80},{112,96},{17,1},{33... | collective-permute-start | bytes 3145736 | tf_op jit(solution)/shard_map/while/body/eval_jaxpr/ppermute | solution.py:15
  385.0 13.7 collective-permute-done
  403.3 37.6 %all-gather.3.cloned.1.call-done = bf16[128,4096]{1,0:T(8,128)(2,1)} async-done(((bf16[128,256]{1,0:T(8,128)(2,1)}), bf16[128,4096]{1,0:T(8,128)(2,1)}) %all-gather.3.cloned.1.call-update) | async-done | bytes 1048592 | tf_op jit(solution)/shard_map/while/body/eval_jaxpr/all_gather | solution.py:73
  446.6 58.4 %psum.31 = f32[128,2,32]{0,2,1:T(8,128)S(1)} all-reduce(f32[128,2,32]{0,2,1:T(8,128)S(1)} %convolution_bitcast_fusion.5), channel_id=1, replica_groups=mesh['section'=8,'tp'=16] {'tp'}, use_global_device_ids=true, to_apply=%region_2.2 | all-reduce | flops 8192 | bytes 65536 | tf_op jit(solution)/shard_map/while/body/eval_jaxpr/psum | solution.py:82
  507.3 17.7 %collective-permute-start = (bf16[128,4096]{1,0:T(8,128)(2,1)}, bf16[128,4096]{1,0:T(8,128)(2,1)S(1)}, u32[]{:S(2)}, u32[]{:S(2)}) collective-permute-start(bf16[128,4096]{1,0:T(8,128)(2,1)} %get-tuple-element.465), channel_id=1, source_target_pairs={{16,0},{32,16},{48,32},{64,48},{80,64},{96,80},{112,96},{17,1},{33... | collective-permute-start | bytes 3145736 | tf_op jit(solution)/shard_map/while/body/eval_jaxpr/ppermute | solution.py:15
  525.0 13.7 collective-permute-done
  543.4 37.6 %all-gather.3.cloned.1.call-done = bf16[128,4096]{1,0:T(8,128)(2,1)} async-done(((bf16[128,256]{1,0:T(8,128)(2,1)}), bf16[128,4096]{1,0:T(8,128)(2,1)}) %all-gather.3.cloned.1.call-update) | async-done | bytes 1048592 | tf_op jit(solution)/shard_map/while/body/eval_jaxpr/all_gather | solution.py:73
  586.7 58.4 %psum.31 = f32[128,2,32]{0,2,1:T(8,128)S(1)} all-reduce(f32[128,2,32]{0,2,1:T(8,128)S(1)} %convolution_bitcast_fusion.5), channel_id=1, replica_groups=mesh['section'=8,'tp'=16] {'tp'}, use_global_device_ids=true, to_apply=%region_2.2 | all-reduce | flops 8192 | bytes 65536 | tf_op jit(solution)/shard_map/while/body/eval_jaxpr/psum | solution.py:82
  647.3 17.7 %collective-permute-start = (bf16[128,4096]{1,0:T(8,128)(2,1)}, bf16[128,4096]{1,0:T(8,128)(2,1)S(1)}, u32[]{:S(2)}, u32[]{:S(2)}) collective-permute-start(bf16[128,4096]{1,0:T(8,128)(2,1)} %get-tuple-element.465), channel_id=1, source_target_pairs={{16,0},{32,16},{48,32},{64,48},{80,64},{96,80},{112,96},{17,1},{33... | collective-permute-start | bytes 3145736 | tf_op jit(solution)/shard_map/while/body/eval_jaxpr/ppermute | solution.py:15
  665.0 13.7 collective-permute-done
  683.4 37.6 %all-gather.3.cloned.1.call-done = bf16[128,4096]{1,0:T(8,128)(2,1)} async-done(((bf16[128,256]{1,0:T(8,128)(2,1)}), bf16[128,4096]{1,0:T(8,128)(2,1)}) %all-gather.3.cloned.1.call-update) | async-done | bytes 1048592 | tf_op jit(solution)/shard_map/while/body/eval_jaxpr/all_gather | solution.py:73
  726.7 58.4 %psum.31 = f32[128,2,32]{0,2,1:T(8,128)S(1)} all-reduce(f32[128,2,32]{0,2,1:T(8,128)S(1)} %convolution_bitcast_fusion.5), channel_id=1, replica_groups=mesh['section'=8,'tp'=16] {'tp'}, use_global_device_ids=true, to_apply=%region_2.2 | all-reduce | flops 8192 | bytes 65536 | tf_op jit(solution)/shard_map/while/body/eval_jaxpr/psum | solution.py:82
  787.3 17.7 %collective-permute-start = (bf16[128,4096]{1,0:T(8,128)(2,1)}, bf16[128,4096]{1,0:T(8,128)(2,1)S(1)}, u32[]{:S(2)}, u32[]{:S(2)}) collective-permute-start(bf16[128,4096]{1,0:T(8,128)(2,1)} %get-tuple-element.465), channel_id=1, source_target_pairs={{16,0},{32,16},{48,32},{64,48},{80,64},{96,80},{112,96},{17,1},{33... | collective-permute-start | bytes 3145736 | tf_op jit(solution)/shard_map/while/body/eval_jaxpr/ppermute | solution.py:15
  805.0 13.7 collective-permute-done
  823.4 37.6 %all-gather.3.cloned.1.call-done = bf16[128,4096]{1,0:T(8,128)(2,1)} async-done(((bf16[128,256]{1,0:T(8,128)(2,1)}), bf16[128,4096]{1,0:T(8,128)(2,1)}) %all-gather.3.cloned.1.call-update) | async-done | bytes 1048592 | tf_op jit(solution)/shard_map/while/body/eval_jaxpr/all_gather | solution.py:73
  866.7 58.4 %psum.31 = f32[128,2,32]{0,2,1:T(8,128)S(1)} all-reduce(f32[128,2,32]{0,2,1:T(8,128)S(1)} %convolution_bitcast_fusion.5), channel_id=1, replica_groups=mesh['section'=8,'tp'=16] {'tp'}, use_global_device_ids=true, to_apply=%region_2.2 | all-reduce | flops 8192 | bytes 65536 | tf_op jit(solution)/shard_map/while/body/eval_jaxpr/psum | solution.py:82
  927.4 17.7 %collective-permute-start = (bf16[128,4096]{1,0:T(8,128)(2,1)}, bf16[128,4096]{1,0:T(8,128)(2,1)S(1)}, u32[]{:S(2)}, u32[]{:S(2)}) collective-permute-start(bf16[128,4096]{1,0:T(8,128)(2,1)} %get-tuple-element.465), channel_id=1, source_target_pairs={{16,0},{32,16},{48,32},{64,48},{80,64},{96,80},{112,96},{17,1},{33... | collective-permute-start | bytes 3145736 | tf_op jit(solution)/shard_map/while/body/eval_jaxpr/ppermute | solution.py:15
  945.1 13.7 collective-permute-done
  963.4 37.6 %all-gather.3.cloned.1.call-done = bf16[128,4096]{1,0:T(8,128)(2,1)} async-done(((bf16[128,256]{1,0:T(8,128)(2,1)}), bf16[128,4096]{1,0:T(8,128)(2,1)}) %all-gather.3.cloned.1.call-update) | async-done | bytes 1048592 | tf_op jit(solution)/shard_map/while/body/eval_jaxpr/all_gather | solution.py:73
  1006.7 58.4 %psum.31 = f32[128,2,32]{0,2,1:T(8,128)S(1)} all-reduce(f32[128,2,32]{0,2,1:T(8,128)S(1)} %convolution_bitcast_fusion.5), channel_id=1, replica_groups=mesh['section'=8,'tp'=16] {'tp'}, use_global_device_ids=true, to_apply=%region_2.2 | all-reduce | flops 8192 | bytes 65536 | tf_op jit(solution)/shard_map/while/body/eval_jaxpr/psum | solution.py:82
  1067.4 17.7 %collective-permute-start = (bf16[128,4096]{1,0:T(8,128)(2,1)}, bf16[128,4096]{1,0:T(8,128)(2,1)S(1)}, u32[]{:S(2)}, u32[]{:S(2)}) collective-permute-start(bf16[128,4096]{1,0:T(8,128)(2,1)} %get-tuple-element.465), channel_id=1, source_target_pairs={{16,0},{32,16},{48,32},{64,48},{80,64},{96,80},{112,96},{17,1},{33... | collective-permute-start | bytes 3145736 | tf_op jit(solution)/shard_map/while/body/eval_jaxpr/ppermute | solution.py:15
  1085.1 13.7 collective-permute-done
  1103.5 37.6 %all-gather.3.cloned.1.call-done = bf16[128,4096]{1,0:T(8,128)(2,1)} async-done(((bf16[128,256]{1,0:T(8,128)(2,1)}), bf16[128,4096]{1,0:T(8,128)(2,1)}) %all-gather.3.cloned.1.call-update) | async-done | bytes 1048592 | tf_op jit(solution)/shard_map/while/body/eval_jaxpr/all_gather | solution.py:73
  1146.8 58.4 %psum.31 = f32[128,2,32]{0,2,1:T(8,128)S(1)} all-reduce(f32[128,2,32]{0,2,1:T(8,128)S(1)} %convolution_bitcast_fusion.5), channel_id=1, replica_groups=mesh['section'=8,'tp'=16] {'tp'}, use_global_device_ids=true, to_apply=%region_2.2 | all-reduce | flops 8192 | bytes 65536 | tf_op jit(solution)/shard_map/while/body/eval_jaxpr/psum | solution.py:82
  1207.4 17.7 %collective-permute-start = (bf16[128,4096]{1,0:T(8,128)(2,1)}, bf16[128,4096]{1,0:T(8,128)(2,1)S(1)}, u32[]{:S(2)}, u32[]{:S(2)}) collective-permute-start(bf16[128,4096]{1,0:T(8,128)(2,1)} %get-tuple-element.465), channel_id=1, source_target_pairs={{16,0},{32,16},{48,32},{64,48},{80,64},{96,80},{112,96},{17,1},{33... | collective-permute-start | bytes 3145736 | tf_op jit(solution)/shard_map/while/body/eval_jaxpr/ppermute | solution.py:15
  1225.1 13.7 collective-permute-done
  1243.5 37.6 %all-gather.3.cloned.1.call-done = bf16[128,4096]{1,0:T(8,128)(2,1)} async-done(((bf16[128,256]{1,0:T(8,128)(2,1)}), bf16[128,4096]{1,0:T(8,128)(2,1)}) %all-gather.3.cloned.1.call-update) | async-done | bytes 1048592 | tf_op jit(solution)/shard_map/while/body/eval_jaxpr/all_gather | solution.py:73
  1286.8 58.4 %psum.31 = f32[128,2,32]{0,2,1:T(8,128)S(1)} all-reduce(f32[128,2,32]{0,2,1:T(8,128)S(1)} %convolution_bitcast_fusion.5), channel_id=1, replica_groups=mesh['section'=8,'tp'=16] {'tp'}, use_global_device_ids=true, to_apply=%region_2.2 | all-reduce | flops 8192 | bytes 65536 | tf_op jit(solution)/shard_map/while/body/eval_jaxpr/psum | solution.py:82
  1347.4 17.7 %collective-permute-start = (bf16[128,4096]{1,0:T(8,128)(2,1)}, bf16[128,4096]{1,0:T(8,128)(2,1)S(1)}, u32[]{:S(2)}, u32[]{:S(2)}) collective-permute-start(bf16[128,4096]{1,0:T(8,128)(2,1)} %get-tuple-element.465), channel_id=1, source_target_pairs={{16,0},{32,16},{48,32},{64,48},{80,64},{96,80},{112,96},{17,1},{33... | collective-permute-start | bytes 3145736 | tf_op jit(solution)/shard_map/while/body/eval_jaxpr/ppermute | solution.py:15
  1365.1 13.7 collective-permute-done
  1383.5 37.6 %all-gather.3.cloned.1.call-done = bf16[128,4096]{1,0:T(8,128)(2,1)} async-done(((bf16[128,256]{1,0:T(8,128)(2,1)}), bf16[128,4096]{1,0:T(8,128)(2,1)}) %all-gather.3.cloned.1.call-update) | async-done | bytes 1048592 | tf_op jit(solution)/shard_map/while/body/eval_jaxpr/all_gather | solution.py:73
  1426.8 58.4 %psum.31 = f32[128,2,32]{0,2,1:T(8,128)S(1)} all-reduce(f32[128,2,32]{0,2,1:T(8,128)S(1)} %convolution_bitcast_fusion.5), channel_id=1, replica_groups=mesh['section'=8,'tp'=16] {'tp'}, use_global_device_ids=true, to_apply=%region_2.2 | all-reduce | flops 8192 | bytes 65536 | tf_op jit(solution)/shard_map/while/body/eval_jaxpr/psum | solution.py:82
  1487.5 17.7 %collective-permute-start = (bf16[128,4096]{1,0:T(8,128)(2,1)}, bf16[128,4096]{1,0:T(8,128)(2,1)S(1)}, u32[]{:S(2)}, u32[]{:S(2)}) collective-permute-start(bf16[128,4096]{1,0:T(8,128)(2,1)} %get-tuple-element.465), channel_id=1, source_target_pairs={{16,0},{32,16},{48,32},{64,48},{80,64},{96,80},{112,96},{17,1},{33... | collective-permute-start | bytes 3145736 | tf_op jit(solution)/shard_map/while/body/eval_jaxpr/ppermute | solution.py:15
  1505.2 13.7 collective-permute-done
  1523.5 37.6 %all-gather.3.cloned.1.call-done = bf16[128,4096]{1,0:T(8,128)(2,1)} async-done(((bf16[128,256]{1,0:T(8,128)(2,1)}), bf16[128,4096]{1,0:T(8,128)(2,1)}) %all-gather.3.cloned.1.call-update) | async-done | bytes 1048592 | tf_op jit(solution)/shard_map/while/body/eval_jaxpr/all_gather | solution.py:73
  1566.8 58.4 %psum.31 = f32[128,2,32]{0,2,1:T(8,128)S(1)} all-reduce(f32[128,2,32]{0,2,1:T(8,128)S(1)} %convolution_bitcast_fusion.5), channel_id=1, replica_groups=mesh['section'=8,'tp'=16] {'tp'}, use_global_device_ids=true, to_apply=%region_2.2 | all-reduce | flops 8192 | bytes 65536 | tf_op jit(solution)/shard_map/while/body/eval_jaxpr/psum | solution.py:82
  1627.8 28.1 %psum.28 = f32[2,32]{1,0:T(2,128)} all-reduce(f32[2,32]{1,0:T(2,128)S(1)} %convolution_bitcast_fusion.3), channel_id=1, replica_groups=mesh['section'=8,'tp'=16] {'section'}, use_global_device_ids=true, to_apply=%region_4.5 | all-reduce | flops 64 | bytes 512 | tf_op jit(solution)/shard_map/psum | solution.py:107
  (201 shorter events, 137.2 us)
Async XLA Ops:
  6.5 1620.9 %copy-start = (bf16[2,32,2048]{2,1,0:T(8,128)(2,1)S(1)}, bf16[2,32,2048]{2,1,0:T(8,128)(2,1)}, u32[]{:S(2)}) copy-start(bf16[2,32,2048]{2,1,0:T(8,128)(2,1)} %param.13) | copy-start | bytes 786436
  6.5 90.4 %all-reduce.2.cloned.1.call-start = ((), (), s32[]{:S(2)}) async-start(), calls=%async_computation | async-start | bytes 524288 | tf_op jit(solution)/shard_map/psum | solution.py:49
  8.8 89.2 %copy-start.3 = (bf16[2,256,32]{1,2,0:T(8,128)(2,1)S(1)}, bf16[2,256,32]{1,2,0:T(8,128)(2,1)}, u32[]{:S(2)}) copy-start(bf16[2,256,32]{1,2,0:T(8,128)(2,1)} %param.12) | copy-start | bytes 98308
  8.8 89.2 %copy-start.4 = (s32[4]{0:T(128)S(1)}, s32[4]{0:T(128)}, u32[]{:S(2)}) copy-start(s32[4]{0:T(128)} %param.15) | copy-start | bytes 52
  98.0 62.9 %all-gather.3.cloned.1.call-start = ((), (), s32[]{:S(2)}) async-start(), calls=%async_computation.1 | async-start | bytes 1114112 | tf_op jit(solution)/shard_map/while/body/eval_jaxpr/all_gather | solution.py:73
  98.0 17.6 %collective-permute-start = (bf16[128,4096]{1,0:T(8,128)(2,1)}, bf16[128,4096]{1,0:T(8,128)(2,1)S(1)}, u32[]{:S(2)}, u32[]{:S(2)}) collective-permute-start(bf16[128,4096]{1,0:T(8,128)(2,1)} %get-tuple-element.465), channel_id=1, source_target_pairs={{16,0},{32,16},{48,32},{64,48},{80,64},{96,80},{112,96},{17,1},{33... | collective-permute-start | bytes 3145736 | tf_op jit(solution)/shard_map/while/body/eval_jaxpr/ppermute | solution.py:15
  120.2 46.2 %copy-start.1 = (bf16[128,256]{1,0:T(8,128)(2,1)S(1)}, bf16[128,256]{1,0:T(8,128)(2,1)}, u32[]{:S(2)}) copy-start(bf16[128,256]{1,0:T(8,128)(2,1)} %add_convert_fusion.4) | copy-start | bytes 196612 | tf_op jit(solution)/shard_map/while
  120.2 106.9 %all-gather.5.cloned.1.call-start = ((), (), s32[]{:S(2)}) async-start(), calls=%async_computation.2 | async-start | bytes 1114112 | tf_op jit(solution)/shard_map/while/body/eval_jaxpr/all_gather | solution.py:77
  227.2 73.7 %all-gather.3.cloned.1.call-start = ((), (), s32[]{:S(2)}) async-start(), calls=%async_computation.1 | async-start | bytes 1114112 | tf_op jit(solution)/shard_map/while/body/eval_jaxpr/all_gather | solution.py:73
  227.2 31.4 %collective-permute-start = (bf16[128,4096]{1,0:T(8,128)(2,1)}, bf16[128,4096]{1,0:T(8,128)(2,1)S(1)}, u32[]{:S(2)}, u32[]{:S(2)}) collective-permute-start(bf16[128,4096]{1,0:T(8,128)(2,1)} %get-tuple-element.465), channel_id=1, source_target_pairs={{16,0},{32,16},{48,32},{64,48},{80,64},{96,80},{112,96},{17,1},{33... | collective-permute-start | bytes 3145736 | tf_op jit(solution)/shard_map/while/body/eval_jaxpr/ppermute | solution.py:15
  263.2 43.2 %copy-start.1 = (bf16[128,256]{1,0:T(8,128)(2,1)S(1)}, bf16[128,256]{1,0:T(8,128)(2,1)}, u32[]{:S(2)}) copy-start(bf16[128,256]{1,0:T(8,128)(2,1)} %add_convert_fusion.4) | copy-start | bytes 196612 | tf_op jit(solution)/shard_map/while
  263.3 103.9 %all-gather.5.cloned.1.call-start = ((), (), s32[]{:S(2)}) async-start(), calls=%async_computation.2 | async-start | bytes 1114112 | tf_op jit(solution)/shard_map/while/body/eval_jaxpr/all_gather | solution.py:77
  367.2 73.8 %all-gather.3.cloned.1.call-start = ((), (), s32[]{:S(2)}) async-start(), calls=%async_computation.1 | async-start | bytes 1114112 | tf_op jit(solution)/shard_map/while/body/eval_jaxpr/all_gather | solution.py:73
  367.3 31.4 %collective-permute-start = (bf16[128,4096]{1,0:T(8,128)(2,1)}, bf16[128,4096]{1,0:T(8,128)(2,1)S(1)}, u32[]{:S(2)}, u32[]{:S(2)}) collective-permute-start(bf16[128,4096]{1,0:T(8,128)(2,1)} %get-tuple-element.465), channel_id=1, source_target_pairs={{16,0},{32,16},{48,32},{64,48},{80,64},{96,80},{112,96},{17,1},{33... | collective-permute-start | bytes 3145736 | tf_op jit(solution)/shard_map/while/body/eval_jaxpr/ppermute | solution.py:15
  403.3 43.2 %copy-start.1 = (bf16[128,256]{1,0:T(8,128)(2,1)S(1)}, bf16[128,256]{1,0:T(8,128)(2,1)}, u32[]{:S(2)}) copy-start(bf16[128,256]{1,0:T(8,128)(2,1)} %add_convert_fusion.4) | copy-start | bytes 196612 | tf_op jit(solution)/shard_map/while
  403.3 103.9 %all-gather.5.cloned.1.call-start = ((), (), s32[]{:S(2)}) async-start(), calls=%async_computation.2 | async-start | bytes 1114112 | tf_op jit(solution)/shard_map/while/body/eval_jaxpr/all_gather | solution.py:77
  507.2 73.8 %all-gather.3.cloned.1.call-start = ((), (), s32[]{:S(2)}) async-start(), calls=%async_computation.1 | async-start | bytes 1114112 | tf_op jit(solution)/shard_map/while/body/eval_jaxpr/all_gather | solution.py:73
  507.3 31.4 %collective-permute-start = (bf16[128,4096]{1,0:T(8,128)(2,1)}, bf16[128,4096]{1,0:T(8,128)(2,1)S(1)}, u32[]{:S(2)}, u32[]{:S(2)}) collective-permute-start(bf16[128,4096]{1,0:T(8,128)(2,1)} %get-tuple-element.465), channel_id=1, source_target_pairs={{16,0},{32,16},{48,32},{64,48},{80,64},{96,80},{112,96},{17,1},{33... | collective-permute-start | bytes 3145736 | tf_op jit(solution)/shard_map/while/body/eval_jaxpr/ppermute | solution.py:15
  543.3 43.2 %copy-start.1 = (bf16[128,256]{1,0:T(8,128)(2,1)S(1)}, bf16[128,256]{1,0:T(8,128)(2,1)}, u32[]{:S(2)}) copy-start(bf16[128,256]{1,0:T(8,128)(2,1)} %add_convert_fusion.4) | copy-start | bytes 196612 | tf_op jit(solution)/shard_map/while
  543.3 103.9 %all-gather.5.cloned.1.call-start = ((), (), s32[]{:S(2)}) async-start(), calls=%async_computation.2 | async-start | bytes 1114112 | tf_op jit(solution)/shard_map/while/body/eval_jaxpr/all_gather | solution.py:77
  647.3 73.8 %all-gather.3.cloned.1.call-start = ((), (), s32[]{:S(2)}) async-start(), calls=%async_computation.1 | async-start | bytes 1114112 | tf_op jit(solution)/shard_map/while/body/eval_jaxpr/all_gather | solution.py:73
  647.3 31.4 %collective-permute-start = (bf16[128,4096]{1,0:T(8,128)(2,1)}, bf16[128,4096]{1,0:T(8,128)(2,1)S(1)}, u32[]{:S(2)}, u32[]{:S(2)}) collective-permute-start(bf16[128,4096]{1,0:T(8,128)(2,1)} %get-tuple-element.465), channel_id=1, source_target_pairs={{16,0},{32,16},{48,32},{64,48},{80,64},{96,80},{112,96},{17,1},{33... | collective-permute-start | bytes 3145736 | tf_op jit(solution)/shard_map/while/body/eval_jaxpr/ppermute | solution.py:15
  683.3 43.2 %copy-start.1 = (bf16[128,256]{1,0:T(8,128)(2,1)S(1)}, bf16[128,256]{1,0:T(8,128)(2,1)}, u32[]{:S(2)}) copy-start(bf16[128,256]{1,0:T(8,128)(2,1)} %add_convert_fusion.4) | copy-start | bytes 196612 | tf_op jit(solution)/shard_map/while
  683.3 103.9 %all-gather.5.cloned.1.call-start = ((), (), s32[]{:S(2)}) async-start(), calls=%async_computation.2 | async-start | bytes 1114112 | tf_op jit(solution)/shard_map/while/body/eval_jaxpr/all_gather | solution.py:77
  787.3 73.8 %all-gather.3.cloned.1.call-start = ((), (), s32[]{:S(2)}) async-start(), calls=%async_computation.1 | async-start | bytes 1114112 | tf_op jit(solution)/shard_map/while/body/eval_jaxpr/all_gather | solution.py:73
  787.3 31.4 %collective-permute-start = (bf16[128,4096]{1,0:T(8,128)(2,1)}, bf16[128,4096]{1,0:T(8,128)(2,1)S(1)}, u32[]{:S(2)}, u32[]{:S(2)}) collective-permute-start(bf16[128,4096]{1,0:T(8,128)(2,1)} %get-tuple-element.465), channel_id=1, source_target_pairs={{16,0},{32,16},{48,32},{64,48},{80,64},{96,80},{112,96},{17,1},{33... | collective-permute-start | bytes 3145736 | tf_op jit(solution)/shard_map/while/body/eval_jaxpr/ppermute | solution.py:15
  823.3 43.2 %copy-start.1 = (bf16[128,256]{1,0:T(8,128)(2,1)S(1)}, bf16[128,256]{1,0:T(8,128)(2,1)}, u32[]{:S(2)}) copy-start(bf16[128,256]{1,0:T(8,128)(2,1)} %add_convert_fusion.4) | copy-start | bytes 196612 | tf_op jit(solution)/shard_map/while
  823.4 103.9 %all-gather.5.cloned.1.call-start = ((), (), s32[]{:S(2)}) async-start(), calls=%async_computation.2 | async-start | bytes 1114112 | tf_op jit(solution)/shard_map/while/body/eval_jaxpr/all_gather | solution.py:77
  927.3 73.8 %all-gather.3.cloned.1.call-start = ((), (), s32[]{:S(2)}) async-start(), calls=%async_computation.1 | async-start | bytes 1114112 | tf_op jit(solution)/shard_map/while/body/eval_jaxpr/all_gather | solution.py:73
  927.4 31.4 %collective-permute-start = (bf16[128,4096]{1,0:T(8,128)(2,1)}, bf16[128,4096]{1,0:T(8,128)(2,1)S(1)}, u32[]{:S(2)}, u32[]{:S(2)}) collective-permute-start(bf16[128,4096]{1,0:T(8,128)(2,1)} %get-tuple-element.465), channel_id=1, source_target_pairs={{16,0},{32,16},{48,32},{64,48},{80,64},{96,80},{112,96},{17,1},{33... | collective-permute-start | bytes 3145736 | tf_op jit(solution)/shard_map/while/body/eval_jaxpr/ppermute | solution.py:15
  963.4 43.2 %copy-start.1 = (bf16[128,256]{1,0:T(8,128)(2,1)S(1)}, bf16[128,256]{1,0:T(8,128)(2,1)}, u32[]{:S(2)}) copy-start(bf16[128,256]{1,0:T(8,128)(2,1)} %add_convert_fusion.4) | copy-start | bytes 196612 | tf_op jit(solution)/shard_map/while
  963.4 103.9 %all-gather.5.cloned.1.call-start = ((), (), s32[]{:S(2)}) async-start(), calls=%async_computation.2 | async-start | bytes 1114112 | tf_op jit(solution)/shard_map/while/body/eval_jaxpr/all_gather | solution.py:77
  1067.3 73.8 %all-gather.3.cloned.1.call-start = ((), (), s32[]{:S(2)}) async-start(), calls=%async_computation.1 | async-start | bytes 1114112 | tf_op jit(solution)/shard_map/while/body/eval_jaxpr/all_gather | solution.py:73
  1067.4 31.4 %collective-permute-start = (bf16[128,4096]{1,0:T(8,128)(2,1)}, bf16[128,4096]{1,0:T(8,128)(2,1)S(1)}, u32[]{:S(2)}, u32[]{:S(2)}) collective-permute-start(bf16[128,4096]{1,0:T(8,128)(2,1)} %get-tuple-element.465), channel_id=1, source_target_pairs={{16,0},{32,16},{48,32},{64,48},{80,64},{96,80},{112,96},{17,1},{33... | collective-permute-start | bytes 3145736 | tf_op jit(solution)/shard_map/while/body/eval_jaxpr/ppermute | solution.py:15
  1103.4 43.2 %copy-start.1 = (bf16[128,256]{1,0:T(8,128)(2,1)S(1)}, bf16[128,256]{1,0:T(8,128)(2,1)}, u32[]{:S(2)}) copy-start(bf16[128,256]{1,0:T(8,128)(2,1)} %add_convert_fusion.4) | copy-start | bytes 196612 | tf_op jit(solution)/shard_map/while
  1103.4 103.9 %all-gather.5.cloned.1.call-start = ((), (), s32[]{:S(2)}) async-start(), calls=%async_computation.2 | async-start | bytes 1114112 | tf_op jit(solution)/shard_map/while/body/eval_jaxpr/all_gather | solution.py:77
  1207.4 73.8 %all-gather.3.cloned.1.call-start = ((), (), s32[]{:S(2)}) async-start(), calls=%async_computation.1 | async-start | bytes 1114112 | tf_op jit(solution)/shard_map/while/body/eval_jaxpr/all_gather | solution.py:73
  1207.4 31.4 %collective-permute-start = (bf16[128,4096]{1,0:T(8,128)(2,1)}, bf16[128,4096]{1,0:T(8,128)(2,1)S(1)}, u32[]{:S(2)}, u32[]{:S(2)}) collective-permute-start(bf16[128,4096]{1,0:T(8,128)(2,1)} %get-tuple-element.465), channel_id=1, source_target_pairs={{16,0},{32,16},{48,32},{64,48},{80,64},{96,80},{112,96},{17,1},{33... | collective-permute-start | bytes 3145736 | tf_op jit(solution)/shard_map/while/body/eval_jaxpr/ppermute | solution.py:15
  1243.4 43.2 %copy-start.1 = (bf16[128,256]{1,0:T(8,128)(2,1)S(1)}, bf16[128,256]{1,0:T(8,128)(2,1)}, u32[]{:S(2)}) copy-start(bf16[128,256]{1,0:T(8,128)(2,1)} %add_convert_fusion.4) | copy-start | bytes 196612 | tf_op jit(solution)/shard_map/while
  1243.4 103.9 %all-gather.5.cloned.1.call-start = ((), (), s32[]{:S(2)}) async-start(), calls=%async_computation.2 | async-start | bytes 1114112 | tf_op jit(solution)/shard_map/while/body/eval_jaxpr/all_gather | solution.py:77
  1347.4 73.8 %all-gather.3.cloned.1.call-start = ((), (), s32[]{:S(2)}) async-start(), calls=%async_computation.1 | async-start | bytes 1114112 | tf_op jit(solution)/shard_map/while/body/eval_jaxpr/all_gather | solution.py:73
  1347.4 31.4 %collective-permute-start = (bf16[128,4096]{1,0:T(8,128)(2,1)}, bf16[128,4096]{1,0:T(8,128)(2,1)S(1)}, u32[]{:S(2)}, u32[]{:S(2)}) collective-permute-start(bf16[128,4096]{1,0:T(8,128)(2,1)} %get-tuple-element.465), channel_id=1, source_target_pairs={{16,0},{32,16},{48,32},{64,48},{80,64},{96,80},{112,96},{17,1},{33... | collective-permute-start | bytes 3145736 | tf_op jit(solution)/shard_map/while/body/eval_jaxpr/ppermute | solution.py:15
  1383.4 43.2 %copy-start.1 = (bf16[128,256]{1,0:T(8,128)(2,1)S(1)}, bf16[128,256]{1,0:T(8,128)(2,1)}, u32[]{:S(2)}) copy-start(bf16[128,256]{1,0:T(8,128)(2,1)} %add_convert_fusion.4) | copy-start | bytes 196612 | tf_op jit(solution)/shard_map/while
  1383.5 103.9 %all-gather.5.cloned.1.call-start = ((), (), s32[]{:S(2)}) async-start(), calls=%async_computation.2 | async-start | bytes 1114112 | tf_op jit(solution)/shard_map/while/body/eval_jaxpr/all_gather | solution.py:77
  1487.4 73.8 %all-gather.3.cloned.1.call-start = ((), (), s32[]{:S(2)}) async-start(), calls=%async_computation.1 | async-start | bytes 1114112 | tf_op jit(solution)/shard_map/while/body/eval_jaxpr/all_gather | solution.py:73
  1487.5 31.4 %collective-permute-start = (bf16[128,4096]{1,0:T(8,128)(2,1)}, bf16[128,4096]{1,0:T(8,128)(2,1)S(1)}, u32[]{:S(2)}, u32[]{:S(2)}) collective-permute-start(bf16[128,4096]{1,0:T(8,128)(2,1)} %get-tuple-element.465), channel_id=1, source_target_pairs={{16,0},{32,16},{48,32},{64,48},{80,64},{96,80},{112,96},{17,1},{33... | collective-permute-start | bytes 3145736 | tf_op jit(solution)/shard_map/while/body/eval_jaxpr/ppermute | solution.py:15
  1523.5 43.2 %copy-start.1 = (bf16[128,256]{1,0:T(8,128)(2,1)S(1)}, bf16[128,256]{1,0:T(8,128)(2,1)}, u32[]{:S(2)}) copy-start(bf16[128,256]{1,0:T(8,128)(2,1)} %add_convert_fusion.4) | copy-start | bytes 196612 | tf_op jit(solution)/shard_map/while
  1523.5 103.9 %all-gather.5.cloned.1.call-start = ((), (), s32[]{:S(2)}) async-start(), calls=%async_computation.2 | async-start | bytes 1114112 | tf_op jit(solution)/shard_map/while/body/eval_jaxpr/all_gather | solution.py:77
  (1 other events, 2.3 us)
Sparse Core Ops, SparseCore 0:
  10.5 86.3 all-reduce.1
  120.3 40.5 all-gather.2
  164.4 42.9 all-gather.4
  263.4 37.5 all-gather.2
  304.4 42.9 all-gather.4
  403.4 37.5 all-gather.2
  444.4 42.9 all-gather.4
  543.4 37.5 all-gather.2
  584.5 42.9 all-gather.4
  683.4 37.5 all-gather.2
  724.5 42.9 all-gather.4
  823.5 37.5 all-gather.2
  864.5 42.9 all-gather.4
  963.5 37.5 all-gather.2
  1004.5 42.9 all-gather.4
  1103.5 37.5 all-gather.2
  1144.6 42.9 all-gather.4
  1243.5 37.5 all-gather.2
  1284.6 42.9 all-gather.4
  1383.6 37.5 all-gather.2
  1424.6 42.9 all-gather.4
  1523.6 37.5 all-gather.2
  1564.6 42.9 all-gather.4
where the time goes:
time: 1660 us
  blocking collectives  671 us (40%)
  waiting for transfers between devices  657 us (40%)
  starting transfers between devices  182 us (11%)
  matrix products  95 us (6%)
  other arithmetic  26.3 us (2%)
  local copies, waits for them, and re-layouts  17.8 us (1%)
    psum x11, blocking collectives, tick(): lax.psum(partial_out.reshape(block_rows, -1), 'tp')  643 us
    all_gather x11, waiting for transfers between devices, tick(): lax.all_gather(middle_own, 'tp', axis=1, tiled=True)  417 us
    ppermute x11, starting transfers between devices, from_behind(): return lax.ppermute(value, axis, pairs)  181 us
    ppermute x11, waiting for transfers between devices, from_behind(): return lax.ppermute(value, axis, pairs)  151 us
    psum x1, waiting for transfers between devices, shards(): lax.psum(partial_in.reshape(total_tokens, -1), 'tp')  87.7 us
    dot_general x11, matrix products, contract_columns(): lax.dot_general(portion, matrix, (((1,), (1,)), ((), ())), preferred_elem...  36.4 us
    dot_general x11, matrix products, tick(): lax.dot_general(upper_full, weights[1], (((1,), (1,)), ((), ())), preferr...  33.7 us
  transfers between devices with their start and end apart: 34, of which 23 were waited for; matrix products, arithmetic and copies ran while one was open for 3% of the time, Pallas kernels for 0%

commit v1 on v0

v1 whole, which is shorter than its diff:
```python
import functools

import jax
import jax.numpy as jnp
from jax import lax
from jax.experimental import pallas as pl
from jax.experimental.pallas import tpu as pltpu
from jax.sharding import Mesh, PartitionSpec as P

AXES = ("x", "c", "z", "y")
SIZES = {"x": 4, "c": 2, "z": 4, "y": 4}
ALL = (0, 1, 2, 3)
SEQ = 128
RIN = 64
ROUT = 32
LANES = 128
EXAMPLES = 2
F32 = jnp.float32
BF16 = jnp.bfloat16
HIGH = lax.Precision.HIGHEST
NT = (((1,), (1,)), ((), ()))


def linear(x, c, z, y):
    return ((x * 2 + c) * 4 + z) * 4 + y


def shift(value, axis, by, planes=ALL):
    at = AXES.index(axis)
    pairs = []
    for x in planes:
        for c in range(2):
            for z in range(4):
                for y in range(4):
                    here = [x, c, z, y]
                    there = list(here)
                    there[at] = (here[at] + by) % SIZES[axis]
                    pairs.append((linear(*there), linear(*here)))
    return lax.ppermute(value, AXES, pairs)


def down(value, plane):
    pairs = []
    for c in range(2):
        for z in range(4):
            for y in range(4):
                pairs.append((linear(plane, c, z, y), linear(plane - 1, c, z, y)))
    return lax.ppermute(value, AXES, pairs)


def ring(pieces, place):
    stacked = jnp.stack(list(pieces) + list(pieces), 0)
    return lax.dynamic_slice_in_dim(stacked, (4 - place) % 4, 4, 0)


def arrange_body(place, source, own, other):
    core = place[0]
    y = place[1]
    for m in range(4):
        for block in range(4):
            start = block * 1024 + ((y + m) % 4) * 256
            to = pl.ds((m * 4 + block) * LANES, LANES)
            mine = pl.multiple_of(start + core * LANES, LANES)
            theirs = pl.multiple_of(start + (1 - core) * LANES, LANES)
            own[0, :, to] = source[0, :, pl.ds(mine, LANES)]
            other[0, :, to] = source[0, :, pl.ds(theirs, LANES)]


def arrange(place, source, swap_rows):
    groups, rows, width = source.shape
    steps = rows // LANES
    if swap_rows:
        own_map = lambda g, r, place: (g, (r + place[0]) % 2, 0)
        other_map = lambda g, r, place: (g, (r + 1 - place[0]) % 2, 0)
    else:
        own_map = other_map = lambda g, r, place: (g, r, 0)
    half = (groups, rows, width // 2)
    return pl.pallas_call(
        arrange_body,
        grid_spec=pltpu.PrefetchScalarGridSpec(
            num_scalar_prefetch=1,
            grid=(groups, steps),
            in_specs=[pl.BlockSpec((1, LANES, width), lambda g, r, place: (g, r, 0))],
            out_specs=[
                pl.BlockSpec((1, LANES, width // 2), own_map),
                pl.BlockSpec((1, LANES, width // 2), other_map),
            ],
        ),
        out_shape=[jax.ShapeDtypeStruct(half, source.dtype)] * 2,
    )(place, source)


def branch_body(place, c0, c1, c2, c3, w0, w1, w2, w3, keep, send, wide, sems):
    z = place[2]
    copies = []
    for k, ref in enumerate((w0, w1, w2, w3)):
        copy = pltpu.make_async_copy(ref, wide.at[k], sems.at[k])
        copy.start()
        copies.append(copy)
    joined = jnp.concatenate([ref[i] for ref in (c0, c1, c2, c3) for i in range(4)], 1)
    for k in range(4):
        copies[k].wait()
        product = lax.dot_general(joined, wide[k], NT, preferred_element_type=F32)
        at = (z + k) % 4
        keep[at] = product[:, :LANES]
        send[at] = product[:, LANES:]


def branch(place, parts, blocks):
    vmem = pl.BlockSpec(memory_space=pltpu.VMEM)
    shape = jax.ShapeDtypeStruct((4, SEQ, LANES), F32)
    rows, depth = blocks[0].shape
    return pl.pallas_call(
        branch_body,
        in_specs=[pl.BlockSpec(memory_space=pltpu.SMEM)]
        + [vmem] * 4
        + [pl.BlockSpec(memory_space=pl.ANY)] * 4,
        out_specs=[vmem, vmem],
        out_shape=[shape, shape],
        scratch_shapes=[
            pltpu.VMEM((4, rows, depth), BF16),
            pltpu.SemaphoreType.DMA((4,)),
        ],
        cost_estimate=pl.CostEstimate(
            flops=2 * SEQ * 4 * rows * depth,
            bytes_accessed=4 * rows * depth * 2,
            transcendentals=0,
        ),
    )(place, *parts, *blocks)


def halves(value, core):
    low, high = value[..., :LANES], value[..., LANES:]
    first = core == 0
    return jnp.where(first, low, high), jnp.where(first, high, low)


def by_layer(own, received, core):
    first = core == 0
    return [jnp.where(first, own[0], received[0]), jnp.where(first, own[1], received[1])] + [
        jnp.where(first, received[0], own[0]),
        jnp.where(first, received[1], own[1]),
    ]


def slope_of(hidden):
    floats = hidden.astype(F32)
    logistic = jax.nn.sigmoid(floats)
    return logistic * (1.0 + floats * (1.0 - logistic))


def activate(hidden):
    floats = hidden.astype(F32)
    return (floats * jax.nn.sigmoid(floats)).astype(BF16)


def shards(
    layer_inputs, weights, input_basis, output_basis, queries, top_cotangent, sequence_example
):
    x = lax.axis_index("x")
    core = lax.axis_index("c")
    z = lax.axis_index("z")
    y = lax.axis_index("y")
    place = jnp.stack([core, y, z]).astype(jnp.int32)

    own_w, other_w = arrange(place, weights, True)
    swapped = [shift(other_w[i], "c", 1) for i in range(2)]
    own_half = by_layer(own_w, swapped, core)

    gathered = [None] * 4

    def fetch(j, planes=ALL):
        return [shift(own_half[j], "z", k, planes) for k in (1, 2, 3)]

    keep_h, send_h = halves(layer_inputs, core)
    basis = jnp.concatenate([input_basis, output_basis], 2)
    basis = jnp.swapaxes(basis, 1, 2)
    keep_b, send_b = halves(basis, core)
    got = shift(jnp.concatenate([send_h, send_b], 1), "c", 1)
    small = jnp.stack(by_layer(jnp.concatenate([keep_h, keep_b], 1), got, core), 0)
    tokens = layer_inputs.shape[1]
    hidden_natural = small[:, :tokens]
    basis_natural = small[:, tokens:]

    def for_row(k):
        row = (z + 4 - k) % 4
        piece = lax.dynamic_slice_in_dim(hidden_natural, row * SEQ, SEQ, 1)
        return jnp.concatenate([piece, basis_natural], 1)

    small_parts = [for_row(0)] + [shift(for_row(k), "z", k) for k in (1, 2, 3)]
    gathered[2] = fetch(2)
    here = ring(small_parts, z)
    hidden = here[:, :, :SEQ]
    in_basis = here[:, :, SEQ : SEQ + RIN]
    out_basis = here[:, :, SEQ + RIN :]

    in_part = jnp.einsum("zjtc,zjrc->jtr", activate(hidden), in_basis, preferred_element_type=F32)
    in_half = in_part + shift(in_part, "c", 1)
    in_feats = in_half + shift(in_half, "y", 1) + shift(in_half, "y", 2) + shift(in_half, "y", 3)

    top_own, _ = arrange(place, top_cotangent[None], False)
    product = lax.dot_general(top_own[0], own_half[3], NT, preferred_element_type=F32)
    total = product[:, :LANES] + shift(product[:, LANES:], "c", 1, (3,))
    column = (z * 4 + y) * 256 + core * LANES
    top_natural = lax.dynamic_slice(top_cotangent, (0, column), (tokens, LANES))
    below_top = (top_natural.astype(F32) + slope_of(hidden_natural[3]) * total).astype(BF16)

    def row_piece(value, k):
        return lax.dynamic_slice_in_dim(value, ((z + 4 - k) % 4) * SEQ, SEQ, 0)

    first = [row_piece(below_top, 0)]
    first += [shift(row_piece(below_top, k), "z", k, (3,)) for k in (1, 2, 3)]
    state = ring(first, z)
    top_here = jnp.stack(
        [
            lax.dynamic_slice(
                top_cotangent, (z * SEQ, b * 1024 + y * 256 + core * LANES), (SEQ, LANES)
            )
            for b in range(4)
        ],
        0,
    )

    order = {2: ((3, (0, 1, 2)), (1, ALL)), 1: ((0, ALL),)}
    out_part = None
    for plane in (3, 2, 1, 0):
        seen = [None] * 4
        for j in (3, 2, 1, 0):
            if plane == 3 and j == 3:
                seen[j] = top_here
                continue
            seen[j] = state
            blocks = [own_half[j]] + gathered[j]
            if plane == 3 and j in order:
                held = [own_half[n] for n, _ in order[j]]
                blocks, held = lax.optimization_barrier((blocks, held))
                for (n, planes), value in zip(order[j], held):
                    gathered[n] = [shift(value, "z", k, planes) for k in (1, 2, 3)]
            parts = [state] + [shift(state, "y", m, (plane,)) for m in (1, 2, 3)]
            keep, send = branch(place, parts, blocks)
            total = keep + shift(send, "c", 1, (plane,))
            state = (state.astype(F32) + slope_of(hidden[:, j]) * total).astype(BF16)
        part = jnp.einsum(
            "jztc,zjrc->jtr", jnp.stack(seen, 0), out_basis, preferred_element_type=F32
        )
        out_part = part if out_part is None else jnp.where(x == plane, part, out_part)
        if plane > 0:
            state = down(state, plane)

    out_half = out_part + shift(out_part, "c", 1)
    out_feats = (
        out_half + shift(out_half, "y", 1) + shift(out_half, "y", 2) + shift(out_half, "y", 3)
    )
    grads = jnp.einsum("jto,jti->joi", out_feats, in_feats, precision=HIGH)
    grads = lax.dynamic_slice_in_dim(grads, 2 * core, 2, 0).reshape(2, ROUT * RIN)
    rows = jnp.stack([grads] + [shift(grads, "z", k) for k in (1, 2, 3)], 1)
    scores = jnp.einsum("lsk,lqk->sq", rows, queries.astype(F32), precision=HIGH)
    examples = jnp.stack([sequence_example[(z + k) % 4] for k in range(4)])
    select = jnp.arange(EXAMPLES, dtype=jnp.int32)[:, None, None] == examples[None, :, None]
    scores = jnp.sum(jnp.where(select, scores[None], 0.0), 1)
    scores = scores + shift(scores, "c", 1)
    return scores + shift(scores, "x", 1) + shift(scores, "x", 2) + shift(scores, "x", 3)


def solution(mesh):
    fine = Mesh(mesh.devices.reshape(4, 2, 4, 4), AXES)
    section = ("x", "c")
    tp = ("z", "y")
    placed = (
        P(section, None, tp),
        P(section, tp, None),
        P(section, tp, None),
        P(section, tp, None),
        P(section, tp, None),
        P(),
        P(),
    )
    return jax.shard_map(
        shards, mesh=fine, in_specs=placed, out_specs=P(None, tp), check_vma=False
    )
```

time: 1660 us -> 594 us (0.36)
  blocking collectives: 671 us -> 0 us
  waiting for transfers between devices: 657 us -> 288 us
  Pallas kernels: 0 us -> 95.8 us
  matrix products: 95 us -> 4.06 us
  starting transfers between devices: 182 us -> 137 us
    psum x12 -> x0, blocking collectives: 671 us -> none  [the longest x11 643 us: tick(): lax.psum(partial_out.reshape(block_rows, -1), 'tp')]
    all_gather x22 -> x0, waiting for transfers between devices: 417 us -> none  [the longest x11 417 us: tick(): lax.all_gather(middle_own, 'tp', axis=1, tiled=True)]
    ppermute x11 -> x96, waiting for transfers between devices: 151 us -> 288 us  [the longest x93 171 us: shift(): return lax.ppermute(value, AXES, pairs)]
    pallas_call x0 -> x16, Pallas kernels: none -> 95.8 us  [the longest x14 84.1 us: branch(): pl.pallas_call(branch_body, in_specs=[pl.BlockSpec(memory_space=pltpu.SME...]
    dot_general x46 -> x8, matrix products: 95 us -> 4.06 us  [the longest x1 1.57 us: shards(): jnp.einsum('zjtc,zjrc->jtr', activate(hidden), in_basis, preferred_elemen...]
    psum x1 -> x0, waiting for transfers between devices: 87.7 us -> none  [shards(): lax.psum(partial_in.reshape(total_tokens, -1), 'tp')]
    ppermute x11 -> x96, starting transfers between devices: 181 us -> 137 us  [the longest x93 134 us: shift(): return lax.ppermute(value, AXES, pairs)]
    unnamed x8 -> x182, local copies, waits for them, and re-layouts: 0.02 us -> 19.3 us
  transfers between devices with their start and end apart: 34 -> 96, of which waited for: 23 -> 29; matrix products, arithmetic and copies ran while one was open for 3% -> 5% of each run, Pallas kernels for 0% -> 7%
where the time goes in v1:
time: 594 us; the launch traced here: 583 us
  waiting for transfers between devices  288 us (48%)
  starting transfers between devices  137 us (23%)
  Pallas kernels  95.8 us (16%)
  other arithmetic  29.1 us (5%)
  local copies, waits for them, and re-layouts  26.4 us (4%)
    ppermute x93, waiting for transfers between devices, shift(): return lax.ppermute(value, AXES, pairs)  171 us
    ppermute x93, starting transfers between devices, shift(): return lax.ppermute(value, AXES, pairs)  134 us
    ppermute x3, waiting for transfers between devices, down(): return lax.ppermute(value, AXES, pairs)  118 us
    pallas_call x14, Pallas kernels, branch(): pl.pallas_call(branch_body, in_specs=[pl.BlockSpec(memory_space=pltpu.SME...  84.1 us
    unnamed x182, local copies, waits for them, and re-layouts  19.3 us
    convert_element_type x13, other arithmetic, shards(): state = (state.astype(F32) + slope_of(hidden[:, j]) * total).astype(BF16)  15.5 us
  transfers between devices with their start and end apart: 96, of which 29 were waited for; matrix products, arithmetic and copies ran while one was open for 5% of the time, Pallas kernels for 7%

profile of v1, /device:TPU:1, one launch (start us, length us, event | category | flops | bytes accessed | tf_op | source)
XLA Modules:
  0.0 583.4 jit_solution(5766379830111155690)
XLA Ops:
  5.4 5.8 %shard_map.74 = (bf16[2,256,2048]{2,1,0:T(8,128)(2,1)}, bf16[2,256,2048]{2,1,0:T(8,128)(2,1)}) custom-call(s32[3]{0:T(128)} %pad_add_fusion.1.place, bf16[2,256,4096]{2,1,0:T(8,128)(2,1)} %source.1), custom_call_target="tpu_custom_call" | custom-call | tf_op jit(solution)/shard_map/pallas_call | solution.py:78
  11.3 2.7 slice_bitcast_fusion
  14.0 9.3 %collective-permute-start.12 = (bf16[256,2048]{1,0:T(8,128)(2,1)}, bf16[256,2048]{1,0:T(8,128)(2,1)S(1)}, u32[]{:S(2)}, u32[]{:S(2)}) collective-permute-start(bf16[256,2048]{1,0:T(8,128)(2,1)} %get-tuple-element.101), channel_id=1, source_target_pairs={{16,0},{17,1},{18,2},{19,3},{20,4},{21,5},{22,6},{23,7},{24,8},{25... | collective-permute-start | bytes 3145736 | tf_op jit(solution)/shard_map/ppermute | solution.py:39
  24.3 5.9 %shard_map.73 = (bf16[1,512,2048]{2,1,0:T(8,128)(2,1)}, bf16[1,512,2048]{2,1,0:T(8,128)(2,1)}) custom-call(s32[3]{0:T(128)} %pad_add_fusion.1.place, bf16[1,512,4096]{2,1,0:T(8,128)(2,1)} %bitcast.158), custom_call_target="tpu_custom_call" | custom-call | tf_op jit(solution)/shard_map/pallas_call | solution.py:78
  31.9 2.7 collective-permute-start.6
  36.1 8.0 %collective-permute-done.6 = bf16[4,224,128]{2,1,0:T(8,128)(2,1)S(1)} collective-permute-done((bf16[4,224,128]{2,1,0:T(8,128)(2,1)S(1)}, bf16[4,224,128]{2,1,0:T(8,128)(2,1)S(1)}, u32[]{:S(2)}, u32[]{:S(2)}) %collective-permute-start.6) | collective-permute-done | bytes 229408 | tf_op jit(solution)/shard_map/ppermute | solution.py:39
  49.9 3.6 collective-permute-start.13
  57.3 40.0 %collective-permute-done.13.w1 = bf16[256,2048]{1,0:T(8,128)(2,1)S(1)} collective-permute-done((bf16[256,2048]{1,0:T(8,128)(2,1)S(1)}, bf16[256,2048]{1,0:T(8,128)(2,1)S(1)}, u32[]{:S(2)}, u32[]{:S(2)}) %collective-permute-start.13) | collective-permute-done | bytes 1048608 | tf_op jit(solution)/shard_map/ppermute | solution.py:39
  97.3 4.6 collective-permute-done.15.w3
  108.2 6.0 %shard_map.75 = (f32[4,128,128]{2,1,0:T(8,128)}, f32[4,128,128]{2,1,0:T(8,128)}) custom-call(s32[3]{0:T(128)} %pad_add_fusion.1.place, bf16[4,128,128]{2,1,0:T(8,128)(2,1)} %copy-done.36, bf16[4,128,128]{2,1,0:T(8,128)(2,1)} %copy-done.49, bf16[4,128,128]{2,1,0:T(8,128)(2,1)} %copy-done.59, bf16[4,128,128]{2,1,0:T(8,128)(2,1)} %collective-permute-done.11.c3, ...), custom_call_target="tpu_custom_call" | custom-call | flops 536870912 | bytes 4194304 | tf_op jit(solution)/shard_map/pallas_call | solution.py:113
  118.4 7.4 %collective-permute-done.20.w1 = bf16[256,2048]{1,0:T(8,128)(2,1)S(1)} collective-permute-done((bf16[256,2048]{1,0:T(8,128)(2,1)S(1)}, bf16[256,2048]{1,0:T(8,128)(2,1)S(1)}, u32[]{:S(2)}, u32[]{:S(2)}) %collective-permute-start.20) | collective-permute-done | bytes 1048608 | tf_op jit(solution)/shard_map/ppermute | solution.py:39
  126.4 24.6 %collective-permute-done.22.w3 = bf16[256,2048]{1,0:T(8,128)(2,1)} collective-permute-done((bf16[256,2048]{1,0:T(8,128)(2,1)S(1)}, bf16[256,2048]{1,0:T(8,128)(2,1)}, u32[]{:S(2)}, u32[]{:S(2)}) %collective-permute-start.22) | collective-permute-done | bytes 1048608 | tf_op jit(solution)/shard_map/ppermute | solution.py:39
  157.3 6.0 %shard_map.76 = (f32[4,128,128]{2,1,0:T(8,128)}, f32[4,128,128]{2,1,0:T(8,128)}) custom-call(s32[3]{0:T(128)} %pad_add_fusion.1.place, bf16[4,128,128]{2,1,0:T(8,128)(2,1)} %copy-done.18, bf16[4,128,128]{2,1,0:T(8,128)(2,1)} %copy-done.50, bf16[4,128,128]{2,1,0:T(8,128)(2,1)} %copy-done.54, bf16[4,128,128]{2,1,0:T(8,128)(2,1)} %collective-permute-done.19.c3, ...), custom_call_target="tpu_custom_call" | custom-call | flops 536870912 | bytes 4194304 | tf_op jit(solution)/shard_map/pallas_call | solution.py:113
  168.0 4.9 collective-permute-start.35
  175.6 2.6 collective-permute-start.37
  179.7 26.6 %collective-permute-done.29.w3 = bf16[256,2048]{1,0:T(8,128)(2,1)} collective-permute-done((bf16[256,2048]{1,0:T(8,128)(2,1)S(1)}, bf16[256,2048]{1,0:T(8,128)(2,1)}, u32[]{:S(2)}, u32[]{:S(2)}) %collective-permute-start.29) | collective-permute-done | bytes 1048608 | tf_op jit(solution)/shard_map/ppermute | solution.py:39
  206.3 6.0 %shard_map.77 = (f32[4,128,128]{2,1,0:T(8,128)}, f32[4,128,128]{2,1,0:T(8,128)}) custom-call(s32[3]{0:T(128)} %pad_add_fusion.1.place, bf16[4,128,128]{2,1,0:T(8,128)(2,1)} %copy-done.12, bf16[4,128,128]{2,1,0:T(8,128)(2,1)} %copy-done.44, bf16[4,128,128]{2,1,0:T(8,128)(2,1)} %collective-permute-done.25.c2, bf16[4,128,128]{2,1,0:T(8,128)(2,1)} %copy-done.45, ...), custom_call_target="tpu_custom_call" | custom-call | flops 536870912 | bytes 4194304 | tf_op jit(solution)/shard_map/pallas_call | solution.py:113
  216.2 4.4 collective-permute-done.35.w1
  221.2 3.5 collective-permute-done.36.w2
  224.7 24.5 %collective-permute-done.37.w3 = bf16[256,2048]{1,0:T(8,128)(2,1)} collective-permute-done((bf16[256,2048]{1,0:T(8,128)(2,1)S(1)}, bf16[256,2048]{1,0:T(8,128)(2,1)}, u32[]{:S(2)}, u32[]{:S(2)}) %collective-permute-start.37) | collective-permute-done | bytes 1048608 | tf_op jit(solution)/shard_map/ppermute | solution.py:39
  250.5 6.0 %shard_map.78 = (f32[4,128,128]{2,1,0:T(8,128)}, f32[4,128,128]{2,1,0:T(8,128)}) custom-call(s32[3]{0:T(128)} %pad_add_fusion.1.place, bf16[4,128,128]{2,1,0:T(8,128)(2,1)} %copy-done.37, bf16[4,128,128]{2,1,0:T(8,128)(2,1)} %copy-done.48, bf16[4,128,128]{2,1,0:T(8,128)(2,1)} %copy-done.53, bf16[4,128,128]{2,1,0:T(8,128)(2,1)} %copy-done.62, ...), custom_call_target="tpu_custom_call" | custom-call | flops 536870912 | bytes 4194304 | tf_op jit(solution)/shard_map/pallas_call | solution.py:113
  261.8 6.0 %shard_map.79 = (f32[4,128,128]{2,1,0:T(8,128)}, f32[4,128,128]{2,1,0:T(8,128)}) custom-call(s32[3]{0:T(128)} %pad_add_fusion.1.place, bf16[4,128,128]{2,1,0:T(8,128)(2,1)} %copy-done.20, bf16[4,128,128]{2,1,0:T(8,128)(2,1)} %copy-done.63, bf16[4,128,128]{2,1,0:T(8,128)(2,1)} %copy-done.71, bf16[4,128,128]{2,1,0:T(8,128)(2,1)} %copy-done.77, ...), custom_call_target="tpu_custom_call" | custom-call | flops 536870912 | bytes 4194304 | tf_op jit(solution)/shard_map/pallas_call | solution.py:113
  273.2 6.0 %shard_map.80 = (f32[4,128,128]{2,1,0:T(8,128)}, f32[4,128,128]{2,1,0:T(8,128)}) custom-call(s32[3]{0:T(128)} %pad_add_fusion.1.place, bf16[4,128,128]{2,1,0:T(8,128)(2,1)} %copy-done.22, bf16[4,128,128]{2,1,0:T(8,128)(2,1)} %copy-done.64, bf16[4,128,128]{2,1,0:T(8,128)(2,1)} %copy-done.72, bf16[4,128,128]{2,1,0:T(8,128)(2,1)} %copy-done.78, ...), custom_call_target="tpu_custom_call" | custom-call | flops 536870912 | bytes 4194304 | tf_op jit(solution)/shard_map/pallas_call | solution.py:113
  284.5 6.0 %shard_map.81 = (f32[4,128,128]{2,1,0:T(8,128)}, f32[4,128,128]{2,1,0:T(8,128)}) custom-call(s32[3]{0:T(128)} %pad_add_fusion.1.place, bf16[4,128,128]{2,1,0:T(8,128)(2,1)} %copy-done.14, bf16[4,128,128]{2,1,0:T(8,128)(2,1)} %copy-done.65, bf16[4,128,128]{2,1,0:T(8,128)(2,1)} %copy-done.73, bf16[4,128,128]{2,1,0:T(8,128)(2,1)} %copy-done.79, ...), custom_call_target="tpu_custom_call" | custom-call | flops 536870912 | bytes 4194304 | tf_op jit(solution)/shard_map/pallas_call | solution.py:113
  296.5 6.0 %shard_map.82 = (f32[4,128,128]{2,1,0:T(8,128)}, f32[4,128,128]{2,1,0:T(8,128)}) custom-call(s32[3]{0:T(128)} %pad_add_fusion.1.place, bf16[4,128,128]{2,1,0:T(8,128)(2,1)} %copy-done.39, bf16[4,128,128]{2,1,0:T(8,128)(2,1)} %copy-done.66, bf16[4,128,128]{2,1,0:T(8,128)(2,1)} %copy-done.74, bf16[4,128,128]{2,1,0:T(8,128)(2,1)} %copy-done.80, ...), custom_call_target="tpu_custom_call" | custom-call | flops 536870912 | bytes 4194304 | tf_op jit(solution)/shard_map/pallas_call | solution.py:113
  307.8 6.0 %shard_map.83 = (f32[4,128,128]{2,1,0:T(8,128)}, f32[4,128,128]{2,1,0:T(8,128)}) custom-call(s32[3]{0:T(128)} %pad_add_fusion.1.place, bf16[4,128,128]{2,1,0:T(8,128)(2,1)} %copy-done.24, bf16[4,128,128]{2,1,0:T(8,128)(2,1)} %copy-done.67, bf16[4,128,128]{2,1,0:T(8,128)(2,1)} %copy-done.75, bf16[4,128,128]{2,1,0:T(8,128)(2,1)} %copy-done.81, ...), custom_call_target="tpu_custom_call" | custom-call | flops 536870912 | bytes 4194304 | tf_op jit(solution)/shard_map/pallas_call | solution.py:113
  319.4 6.0 %shard_map.84 = (f32[4,128,128]{2,1,0:T(8,128)}, f32[4,128,128]{2,1,0:T(8,128)}) custom-call(s32[3]{0:T(128)} %pad_add_fusion.1.place, bf16[4,128,128]{2,1,0:T(8,128)(2,1)} %copy-done.26, bf16[4,128,128]{2,1,0:T(8,128)(2,1)} %copy-done.68, bf16[4,128,128]{2,1,0:T(8,128)(2,1)} %copy-done.76, bf16[4,128,128]{2,1,0:T(8,128)(2,1)} %copy-done.82, ...), custom_call_target="tpu_custom_call" | custom-call | flops 536870912 | bytes 4194304 | tf_op jit(solution)/shard_map/pallas_call | solution.py:113
  330.7 6.0 %shard_map.85 = (f32[4,128,128]{2,1,0:T(8,128)}, f32[4,128,128]{2,1,0:T(8,128)}) custom-call(s32[3]{0:T(128)} %pad_add_fusion.1.place, bf16[4,128,128]{2,1,0:T(8,128)(2,1)} %copy-done.16, bf16[4,128,128]{2,1,0:T(8,128)(2,1)} %copy-done.55, bf16[4,128,128]{2,1,0:T(8,128)(2,1)} %copy-done.60, bf16[4,128,128]{2,1,0:T(8,128)(2,1)} %copy-done.69, ...), custom_call_target="tpu_custom_call" | custom-call | flops 536870912 | bytes 4194304 | tf_op jit(solution)/shard_map/pallas_call | solution.py:113
  339.9 117.7 %collective-permute-done.68.c0 = bf16[4,128,128]{2,1,0:T(8,128)(2,1)S(1)} collective-permute-done((bf16[4,128,128]{2,1,0:T(8,128)(2,1)S(1)}, bf16[4,128,128]{2,1,0:T(8,128)(2,1)S(1)}, u32[]{:S(2)}, u32[]{:S(2)}) %collective-permute-start.68) | collective-permute-done | bytes 131104 | tf_op jit(solution)/shard_map/ppermute | solution.py:48
  457.6 2.5 collective-permute-start.69
  462.0 2.8 collective-permute-start.71
  467.3 3.9 collective-permute-done.71.c3
  471.9 6.0 %shard_map.86 = (f32[4,128,128]{2,1,0:T(8,128)}, f32[4,128,128]{2,1,0:T(8,128)}) custom-call(s32[3]{0:T(128)} %pad_add_fusion.1.place, bf16[4,128,128]{2,1,0:T(8,128)(2,1)} %copy-done.41, bf16[4,128,128]{2,1,0:T(8,128)(2,1)} %copy-done.56, bf16[4,128,128]{2,1,0:T(8,128)(2,1)} %copy-done.61, bf16[4,128,128]{2,1,0:T(8,128)(2,1)} %copy-done.70, ...), custom_call_target="tpu_custom_call" | custom-call | flops 536870912 | bytes 4194304 | tf_op jit(solution)/shard_map/pallas_call | solution.py:113
  477.9 3.2 collective-permute-start.72
  483.6 3.0 collective-permute-start.73
  494.4 3.8 collective-permute-done.75.c3
  498.9 6.0 %shard_map.87 = (f32[4,128,128]{2,1,0:T(8,128)}, f32[4,128,128]{2,1,0:T(8,128)}) custom-call(s32[3]{0:T(128)} %pad_add_fusion.1.place, bf16[4,128,128]{2,1,0:T(8,128)(2,1)} %copy-done.28, bf16[4,128,128]{2,1,0:T(8,128)(2,1)} %copy-done.46, bf16[4,128,128]{2,1,0:T(8,128)(2,1)} %copy-done.51, bf16[4,128,128]{2,1,0:T(8,128)(2,1)} %copy-done.57, ...), custom_call_target="tpu_custom_call" | custom-call | flops 536870912 | bytes 4194304 | tf_op jit(solution)/shard_map/pallas_call | solution.py:113
  504.9 2.5 collective-permute-start.76
  510.0 4.3 collective-permute-start.77
  519.1 3.1 collective-permute-done.78.c2
  522.2 3.5 collective-permute-done.79.c3
  526.4 6.0 %shard_map.88 = (f32[4,128,128]{2,1,0:T(8,128)}, f32[4,128,128]{2,1,0:T(8,128)}) custom-call(s32[3]{0:T(128)} %pad_add_fusion.1.place, bf16[4,128,128]{2,1,0:T(8,128)(2,1)} %copy-done.30, bf16[4,128,128]{2,1,0:T(8,128)(2,1)} %copy-done.47, bf16[4,128,128]{2,1,0:T(8,128)(2,1)} %copy-done.52, bf16[4,128,128]{2,1,0:T(8,128)(2,1)} %copy-done.58, ...), custom_call_target="tpu_custom_call" | custom-call | flops 536870912 | bytes 4194304 | tf_op jit(solution)/shard_map/pallas_call | solution.py:113
  532.4 2.8 collective-permute-start.80
  544.3 2.5 pad_add_fusion
  553.7 2.6 collective-permute-start.92
  557.2 5.1 collective-permute-start.95
  562.3 8.9 %collective-permute-start.94 = (f32[2,32]{1,0:T(2,128)S(1)}, f32[2,32]{1,0:T(2,128)S(1)}, u32[]{:S(2)}, u32[]{:S(2)}) collective-permute-start(f32[2,32]{1,0:T(2,128)S(1)} %add.389), channel_id=1, source_target_pairs={{64,0},{65,1},{66,2},{67,3},{68,4},{69,5},{70,6},{71,7},{72,8},{73... | collective-permute-start | bytes 776 | tf_op jit(solution)/shard_map/ppermute | solution.py:39
  571.2 8.9 %collective-permute-start.93 = (f32[2,32]{1,0:T(2,128)S(1)}, f32[2,32]{1,0:T(2,128)S(1)}, u32[]{:S(2)}, u32[]{:S(2)}) collective-permute-start(f32[2,32]{1,0:T(2,128)S(1)} %add.389), channel_id=1, source_target_pairs={{32,0},{33,1},{34,2},{35,3},{36,4},{37,5},{38,6},{39,7},{40,8},{41... | collective-permute-start | bytes 776 | tf_op jit(solution)/shard_map/ppermute | solution.py:39
  (403 shorter events, 134.9 us)
Async XLA Ops:
  3.4 26.7 %collective-permute-start = (bf16[2,608,128]{2,1,0:T(8,128)(2,1)}, bf16[2,608,128]{2,1,0:T(8,128)(2,1)}, u32[]{:S(2)}, u32[]{:S(2)}) collective-permute-start(bf16[2,608,128]{2,1,0:T(8,128)(2,1)} %pad_maximum_fusion.1), channel_id=1, source_target_pairs={{16,0},{17,1},{18,2},{19,3},{20,4},{21,5},{22,6},{23,7},{24,8},{25... | collective-permute-start | bytes 933896 | tf_op jit(solution)/shard_map/ppermute | solution.py:39
  14.0 30.9 %collective-permute-start.12 = (bf16[256,2048]{1,0:T(8,128)(2,1)}, bf16[256,2048]{1,0:T(8,128)(2,1)S(1)}, u32[]{:S(2)}, u32[]{:S(2)}) collective-permute-start(bf16[256,2048]{1,0:T(8,128)(2,1)} %get-tuple-element.101), channel_id=1, source_target_pairs={{16,0},{17,1},{18,2},{19,3},{20,4},{21,5},{22,6},{23,7},{24,8},{25... | collective-permute-start | bytes 3145736 | tf_op jit(solution)/shard_map/ppermute | solution.py:39
  23.3 21.6 %collective-permute-start.1 = (bf16[256,2048]{1,0:T(8,128)(2,1)S(1)}, bf16[256,2048]{1,0:T(8,128)(2,1)S(1)}, u32[]{:S(2)}, u32[]{:S(2)}) collective-permute-start(bf16[256,2048]{1,0:T(8,128)(2,1)S(1)} %get-tuple-element.102), channel_id=1, source_target_pairs={{16,0},{17,1},{18,2},{19,3},{20,4},{21,5},{22,6},{23,7},{24,8},{25... | collective-permute-start | bytes 3145736 | tf_op jit(solution)/shard_map/ppermute | solution.py:39
  31.9 12.3 %collective-permute-start.6 = (bf16[4,224,128]{2,1,0:T(8,128)(2,1)S(1)}, bf16[4,224,128]{2,1,0:T(8,128)(2,1)S(1)}, u32[]{:S(2)}, u32[]{:S(2)}) collective-permute-start(bf16[4,224,128]{2,1,0:T(8,128)(2,1)S(1)} %get-tuple-element.114), channel_id=1, source_target_pairs={{4,0},{5,1},{6,2},{7,3},{8,4},{9,5},{10,6},{11,7},{12,8},{13,9},{1... | collective-permute-start | bytes 688136 | tf_op jit(solution)/shard_map/ppermute | solution.py:39
  34.5 13.8 %collective-permute-start.7 = (bf16[4,224,128]{2,1,0:T(8,128)(2,1)S(1)}, bf16[4,224,128]{2,1,0:T(8,128)(2,1)S(1)}, u32[]{:S(2)}, u32[]{:S(2)}) collective-permute-start(bf16[4,224,128]{2,1,0:T(8,128)(2,1)S(1)} %get-tuple-element.113), channel_id=1, source_target_pairs={{8,0},{9,1},{10,2},{11,3},{12,4},{13,5},{14,6},{15,7},{0,8},{1,9},... | collective-permute-start | bytes 688136 | tf_op jit(solution)/shard_map/ppermute | solution.py:39
  34.6 14.4 %collective-permute-start.8 = (bf16[4,224,128]{2,1,0:T(8,128)(2,1)S(1)}, bf16[4,224,128]{2,1,0:T(8,128)(2,1)S(1)}, u32[]{:S(2)}, u32[]{:S(2)}) collective-permute-start(bf16[4,224,128]{2,1,0:T(8,128)(2,1)S(1)} %get-tuple-element.89), channel_id=1, source_target_pairs={{12,0},{13,1},{14,2},{15,3},{0,4},{1,5},{2,6},{3,7},{4,8},{5,9},{6... | collective-permute-start | bytes 688136 | tf_op jit(solution)/shard_map/ppermute | solution.py:39
  47.6 6.4 %collective-permute-start.2 = (f32[512,128]{1,0:T(8,128)S(1)}, f32[512,128]{1,0:T(8,128)S(1)}, u32[]{:S(2)}, u32[]{:S(2)}) collective-permute-start(f32[512,128]{1,0:T(8,128)S(1)} %slice.125), channel_id=1, source_target_pairs={{112,96},{113,97},{114,98},{115,99},{116,100},{117,101},{118,102},... | collective-permute-start | bytes 786440 | tf_op jit(solution)/shard_map/ppermute | solution.py:39
  49.9 47.4 %collective-permute-start.13 = (bf16[256,2048]{1,0:T(8,128)(2,1)S(1)}, bf16[256,2048]{1,0:T(8,128)(2,1)S(1)}, u32[]{:S(2)}, u32[]{:S(2)}) collective-permute-start(bf16[256,2048]{1,0:T(8,128)(2,1)S(1)} %get-tuple-element.50.w0), channel_id=1, source_target_pairs={{4,0},{5,1},{6,2},{7,3},{8,4},{9,5},{10,6},{11,7},{12,8},{13,9},{1... | collective-permute-start | bytes 3145736 | tf_op jit(solution)/shard_map/ppermute | solution.py:39
  53.4 43.8 %collective-permute-start.14 = (bf16[256,2048]{1,0:T(8,128)(2,1)S(1)}, bf16[256,2048]{1,0:T(8,128)(2,1)S(1)}, u32[]{:S(2)}, u32[]{:S(2)}) collective-permute-start(bf16[256,2048]{1,0:T(8,128)(2,1)S(1)} %get-tuple-element.50.w0), channel_id=1, source_target_pairs={{8,0},{9,1},{10,2},{11,3},{12,4},{13,5},{14,6},{15,7},{0,8},{1,9},... | collective-permute-start | bytes 3145736 | tf_op jit(solution)/shard_map/ppermute | solution.py:39
  53.4 48.4 %collective-permute-start.15 = (bf16[256,2048]{1,0:T(8,128)(2,1)S(1)}, bf16[256,2048]{1,0:T(8,128)(2,1)S(1)}, u32[]{:S(2)}, u32[]{:S(2)}) collective-permute-start(bf16[256,2048]{1,0:T(8,128)(2,1)S(1)} %get-tuple-element.50.w0), channel_id=1, source_target_pairs={{12,0},{13,1},{14,2},{15,3},{0,4},{1,5},{2,6},{3,7},{4,8},{5,9},{6... | collective-permute-start | bytes 3145736 | tf_op jit(solution)/shard_map/ppermute | solution.py:39
  101.9 23.9 %collective-permute-start.20 = (bf16[256,2048]{1,0:T(8,128)(2,1)S(1)}, bf16[256,2048]{1,0:T(8,128)(2,1)S(1)}, u32[]{:S(2)}, u32[]{:S(2)}) collective-permute-start(bf16[256,2048]{1,0:T(8,128)(2,1)S(1)} %get-tuple-element.57.w0), channel_id=1, source_target_pairs={{4,0},{5,1},{6,2},{7,3},{8,4},{9,5},{10,6},{11,7},{12,8},{13,9},{1... | collective-permute-start | bytes 3145736 | tf_op jit(solution)/shard_map/ppermute | solution.py:39
  101.9 24.6 %collective-permute-start.21 = (bf16[256,2048]{1,0:T(8,128)(2,1)S(1)}, bf16[256,2048]{1,0:T(8,128)(2,1)}, u32[]{:S(2)}, u32[]{:S(2)}) collective-permute-start(bf16[256,2048]{1,0:T(8,128)(2,1)S(1)} %get-tuple-element.57.w0), channel_id=1, source_target_pairs={{8,0},{9,1},{10,2},{11,3},{12,4},{13,5},{14,6},{15,7},{0,8},{1,9},... | collective-permute-start | bytes 3145736 | tf_op jit(solution)/shard_map/ppermute | solution.py:39
  102.5 48.5 %collective-permute-start.22 = (bf16[256,2048]{1,0:T(8,128)(2,1)S(1)}, bf16[256,2048]{1,0:T(8,128)(2,1)}, u32[]{:S(2)}, u32[]{:S(2)}) collective-permute-start(bf16[256,2048]{1,0:T(8,128)(2,1)S(1)} %get-tuple-element.57.w0), channel_id=1, source_target_pairs={{12,0},{13,1},{14,2},{15,3},{0,4},{1,5},{2,6},{3,7},{4,8},{5,9},{6... | collective-permute-start | bytes 3145736 | tf_op jit(solution)/shard_map/ppermute | solution.py:39
  114.2 36.8 %collective-permute-start.16 = (f32[4,128,128]{2,1,0:T(8,128)}, f32[4,128,128]{2,1,0:T(8,128)S(1)}, u32[]{:S(2)}, u32[]{:S(2)}) collective-permute-start(f32[4,128,128]{2,1,0:T(8,128)} %get-tuple-element.55), channel_id=1, source_target_pairs={{112,96},{113,97},{114,98},{115,99},{116,100},{117,101},{118,102},... | collective-permute-start | bytes 786440 | tf_op jit(solution)/shard_map/ppermute | solution.py:39
  151.0 24.6 %collective-permute-start.27 = (bf16[256,2048]{1,0:T(8,128)(2,1)}, bf16[256,2048]{1,0:T(8,128)(2,1)}, u32[]{:S(2)}, u32[]{:S(2)}) collective-permute-start(bf16[256,2048]{1,0:T(8,128)(2,1)} %get-tuple-element.63.w0), channel_id=1, source_target_pairs={{4,0},{5,1},{6,2},{7,3},{8,4},{9,5},{10,6},{11,7},{12,8},{13,9},{1... | collective-permute-start | bytes 3145736 | tf_op jit(solution)/shard_map/ppermute | solution.py:39
  155.1 24.6 %collective-permute-start.28 = (bf16[256,2048]{1,0:T(8,128)(2,1)S(1)}, bf16[256,2048]{1,0:T(8,128)(2,1)}, u32[]{:S(2)}, u32[]{:S(2)}) collective-permute-start(bf16[256,2048]{1,0:T(8,128)(2,1)S(1)} %copy-done.9), channel_id=1, source_target_pairs={{8,0},{9,1},{10,2},{11,3},{12,4},{13,5},{14,6},{15,7},{0,8},{1,9},... | collective-permute-start | bytes 3145736 | tf_op jit(solution)/shard_map/ppermute | solution.py:39
  155.7 50.5 %collective-permute-start.29 = (bf16[256,2048]{1,0:T(8,128)(2,1)S(1)}, bf16[256,2048]{1,0:T(8,128)(2,1)}, u32[]{:S(2)}, u32[]{:S(2)}) collective-permute-start(bf16[256,2048]{1,0:T(8,128)(2,1)S(1)} %copy-done.9), channel_id=1, source_target_pairs={{12,0},{13,1},{14,2},{15,3},{0,4},{1,5},{2,6},{3,7},{4,8},{5,9},{6... | collective-permute-start | bytes 3145736 | tf_op jit(solution)/shard_map/ppermute | solution.py:39
  167.3 5.6 collective-permute-start.26
  168.0 52.5 %collective-permute-start.35 = (bf16[256,2048]{1,0:T(8,128)(2,1)S(1)}, bf16[256,2048]{1,0:T(8,128)(2,1)S(1)}, u32[]{:S(2)}, u32[]{:S(2)}) collective-permute-start(bf16[256,2048]{1,0:T(8,128)(2,1)S(1)} %copy-done.8), channel_id=1, source_target_pairs={{4,0},{5,1},{6,2},{7,3},{8,4},{9,5},{10,6},{11,7},{12,8},{13,9},{1... | collective-permute-start | bytes 3145736 | tf_op jit(solution)/shard_map/ppermute | solution.py:39
  172.9 51.8 %collective-permute-start.36 = (bf16[256,2048]{1,0:T(8,128)(2,1)S(1)}, bf16[256,2048]{1,0:T(8,128)(2,1)}, u32[]{:S(2)}, u32[]{:S(2)}) collective-permute-start(bf16[256,2048]{1,0:T(8,128)(2,1)S(1)} %copy-done.8), channel_id=1, source_target_pairs={{8,0},{9,1},{10,2},{11,3},{12,4},{13,5},{14,6},{15,7},{0,8},{1,9},... | collective-permute-start | bytes 3145736 | tf_op jit(solution)/shard_map/ppermute | solution.py:39
  175.6 73.6 %collective-permute-start.37 = (bf16[256,2048]{1,0:T(8,128)(2,1)S(1)}, bf16[256,2048]{1,0:T(8,128)(2,1)}, u32[]{:S(2)}, u32[]{:S(2)}) collective-permute-start(bf16[256,2048]{1,0:T(8,128)(2,1)S(1)} %copy-done.8), channel_id=1, source_target_pairs={{12,0},{13,1},{14,2},{15,3},{0,4},{1,5},{2,6},{3,7},{4,8},{5,9},{6... | collective-permute-start | bytes 3145736 | tf_op jit(solution)/shard_map/ppermute | solution.py:39
  214.8 34.3 %collective-permute-start.32 = (bf16[4,128,128]{2,1,0:T(8,128)(2,1)S(1)}, bf16[4,128,128]{2,1,0:T(8,128)(2,1)S(1)}, u32[]{:S(2)}, u32[]{:S(2)}) collective-permute-start(bf16[4,128,128]{2,1,0:T(8,128)(2,1)S(1)} %collective-permute-done.31.c0), channel_id=1, source_target_pairs={{65,64},{66,65},{67,66},{64,67},{69,68},{70,69},{71,70},{68,71},{7... | collective-permute-start | bytes 393224 | tf_op jit(solution)/shard_map/ppermute | solution.py:39
  215.5 33.7 %collective-permute-start.33 = (bf16[4,128,128]{2,1,0:T(8,128)(2,1)S(1)}, bf16[4,128,128]{2,1,0:T(8,128)(2,1)S(1)}, u32[]{:S(2)}, u32[]{:S(2)}) collective-permute-start(bf16[4,128,128]{2,1,0:T(8,128)(2,1)S(1)} %collective-permute-done.31.c0), channel_id=1, source_target_pairs={{66,64},{67,65},{64,66},{65,67},{70,68},{71,69},{68,70},{69,71},{7... | collective-permute-start | bytes 393224 | tf_op jit(solution)/shard_map/ppermute | solution.py:39
  220.6 28.6 %collective-permute-start.34 = (bf16[4,128,128]{2,1,0:T(8,128)(2,1)S(1)}, bf16[4,128,128]{2,1,0:T(8,128)(2,1)S(1)}, u32[]{:S(2)}, u32[]{:S(2)}) collective-permute-start(bf16[4,128,128]{2,1,0:T(8,128)(2,1)S(1)} %collective-permute-done.31.c0), channel_id=1, source_target_pairs={{67,64},{64,65},{65,66},{66,67},{71,68},{68,69},{69,70},{70,71},{7... | collective-permute-start | bytes 393224 | tf_op jit(solution)/shard_map/ppermute | solution.py:39
  338.6 119.0 %collective-permute-start.68 = (bf16[4,128,128]{2,1,0:T(8,128)(2,1)S(1)}, bf16[4,128,128]{2,1,0:T(8,128)(2,1)S(1)}, u32[]{:S(2)}, u32[]{:S(2)}) collective-permute-start(bf16[4,128,128]{2,1,0:T(8,128)(2,1)S(1)} %add_convert_fusion.3), channel_id=1, source_target_pairs={{32,0},{33,1},{34,2},{35,3},{36,4},{37,5},{38,6},{39,7},{40,8},{41... | collective-permute-start | bytes 393224 | tf_op jit(solution)/shard_map/ppermute | solution.py:48
  457.6 7.2 %collective-permute-start.69 = (bf16[4,128,128]{2,1,0:T(8,128)(2,1)S(1)}, bf16[4,128,128]{2,1,0:T(8,128)(2,1)S(1)}, u32[]{:S(2)}, u32[]{:S(2)}) collective-permute-start(bf16[4,128,128]{2,1,0:T(8,128)(2,1)S(1)} %collective-permute-done.68.c0), channel_id=1, source_target_pairs={{1,0},{2,1},{3,2},{0,3},{5,4},{6,5},{7,6},{4,7},{9,8},{10,9},{11,1... | collective-permute-start | bytes 393224 | tf_op jit(solution)/shard_map/ppermute | solution.py:39
  460.1 7.2 %collective-permute-start.70 = (bf16[4,128,128]{2,1,0:T(8,128)(2,1)S(1)}, bf16[4,128,128]{2,1,0:T(8,128)(2,1)S(1)}, u32[]{:S(2)}, u32[]{:S(2)}) collective-permute-start(bf16[4,128,128]{2,1,0:T(8,128)(2,1)S(1)} %collective-permute-done.68.c0), channel_id=1, source_target_pairs={{2,0},{3,1},{0,2},{1,3},{6,4},{7,5},{4,6},{5,7},{10,8},{11,9},{8,1... | collective-permute-start | bytes 393224 | tf_op jit(solution)/shard_map/ppermute | solution.py:39
  462.0 9.1 %collective-permute-start.71 = (bf16[4,128,128]{2,1,0:T(8,128)(2,1)S(1)}, bf16[4,128,128]{2,1,0:T(8,128)(2,1)S(1)}, u32[]{:S(2)}, u32[]{:S(2)}) collective-permute-start(bf16[4,128,128]{2,1,0:T(8,128)(2,1)S(1)} %collective-permute-done.68.c0), channel_id=1, source_target_pairs={{3,0},{0,1},{1,2},{2,3},{7,4},{4,5},{5,6},{6,7},{11,8},{8,9},{9,10... | collective-permute-start | bytes 393224 | tf_op jit(solution)/shard_map/ppermute | solution.py:39
  477.9 4.5 collective-permute-start.72
  483.6 10.3 %collective-permute-start.73 = (bf16[4,128,128]{2,1,0:T(8,128)(2,1)S(1)}, bf16[4,128,128]{2,1,0:T(8,128)(2,1)S(1)}, u32[]{:S(2)}, u32[]{:S(2)}) collective-permute-start(bf16[4,128,128]{2,1,0:T(8,128)(2,1)S(1)} %add_convert_fusion.2.c0), channel_id=1, source_target_pairs={{1,0},{2,1},{3,2},{0,3},{5,4},{6,5},{7,6},{4,7},{9,8},{10,9},{11,1... | collective-permute-start | bytes 393224 | tf_op jit(solution)/shard_map/ppermute | solution.py:39
  486.6 7.8 %collective-permute-start.74 = (bf16[4,128,128]{2,1,0:T(8,128)(2,1)S(1)}, bf16[4,128,128]{2,1,0:T(8,128)(2,1)S(1)}, u32[]{:S(2)}, u32[]{:S(2)}) collective-permute-start(bf16[4,128,128]{2,1,0:T(8,128)(2,1)S(1)} %add_convert_fusion.2.c0), channel_id=1, source_target_pairs={{2,0},{3,1},{0,2},{1,3},{6,4},{7,5},{4,6},{5,7},{10,8},{11,9},{8,1... | collective-permute-start | bytes 393224 | tf_op jit(solution)/shard_map/ppermute | solution.py:39
  488.6 9.7 %collective-permute-start.75 = (bf16[4,128,128]{2,1,0:T(8,128)(2,1)S(1)}, bf16[4,128,128]{2,1,0:T(8,128)(2,1)S(1)}, u32[]{:S(2)}, u32[]{:S(2)}) collective-permute-start(bf16[4,128,128]{2,1,0:T(8,128)(2,1)S(1)} %add_convert_fusion.2.c0), channel_id=1, source_target_pairs={{3,0},{0,1},{1,2},{2,3},{7,4},{4,5},{5,6},{6,7},{11,8},{8,9},{9,10... | collective-permute-start | bytes 393224 | tf_op jit(solution)/shard_map/ppermute | solution.py:39
  492.6 15.8 %collective-permute-start.85 = (f32[4,128,64]{1,2,0:T(8,128)S(1)}, f32[4,128,64]{1,2,0:T(8,128)S(1)}, u32[]{:S(2)}, u32[]{:S(2)}) collective-permute-start(f32[4,128,64]{1,2,0:T(8,128)S(1)} %convolution_bitcast_fusion), channel_id=1, source_target_pairs={{16,0},{17,1},{18,2},{19,3},{20,4},{21,5},{22,6},{23,7},{24,8},{25... | collective-permute-start | bytes 393224 | tf_op jit(solution)/shard_map/ppermute | solution.py:39
  508.5 35.0 %collective-permute-start.88 = (f32[4,128,64]{1,2,0:T(8,128)S(1)}, f32[4,128,64]{1,2,0:T(8,128)S(1)}, u32[]{:S(2)}, u32[]{:S(2)}) collective-permute-start(f32[4,128,64]{1,2,0:T(8,128)S(1)} %add.384), channel_id=1, source_target_pairs={{3,0},{0,1},{1,2},{2,3},{7,4},{4,5},{5,6},{6,7},{11,8},{8,9},{9,10... | collective-permute-start | bytes 393224 | tf_op jit(solution)/shard_map/ppermute | solution.py:39
  510.0 9.1 %collective-permute-start.77 = (bf16[4,128,128]{2,1,0:T(8,128)(2,1)S(1)}, bf16[4,128,128]{2,1,0:T(8,128)(2,1)S(1)}, u32[]{:S(2)}, u32[]{:S(2)}) collective-permute-start(bf16[4,128,128]{2,1,0:T(8,128)(2,1)S(1)} %add_convert_fusion.1.c0), channel_id=1, source_target_pairs={{1,0},{2,1},{3,2},{0,3},{5,4},{6,5},{7,6},{4,7},{9,8},{10,9},{11,1... | collective-permute-start | bytes 393224 | tf_op jit(solution)/shard_map/ppermute | solution.py:39
  514.4 7.9 %collective-permute-start.78 = (bf16[4,128,128]{2,1,0:T(8,128)(2,1)S(1)}, bf16[4,128,128]{2,1,0:T(8,128)(2,1)S(1)}, u32[]{:S(2)}, u32[]{:S(2)}) collective-permute-start(bf16[4,128,128]{2,1,0:T(8,128)(2,1)S(1)} %add_convert_fusion.1.c0), channel_id=1, source_target_pairs={{2,0},{3,1},{0,2},{1,3},{6,4},{7,5},{4,6},{5,7},{10,8},{11,9},{8,1... | collective-permute-start | bytes 393224 | tf_op jit(solution)/shard_map/ppermute | solution.py:39
  516.3 9.4 %collective-permute-start.79 = (bf16[4,128,128]{2,1,0:T(8,128)(2,1)S(1)}, bf16[4,128,128]{2,1,0:T(8,128)(2,1)S(1)}, u32[]{:S(2)}, u32[]{:S(2)}) collective-permute-start(bf16[4,128,128]{2,1,0:T(8,128)(2,1)S(1)} %add_convert_fusion.1.c0), channel_id=1, source_target_pairs={{3,0},{0,1},{1,2},{2,3},{7,4},{4,5},{5,6},{6,7},{11,8},{8,9},{9,10... | collective-permute-start | bytes 393224 | tf_op jit(solution)/shard_map/ppermute | solution.py:39
  532.4 4.2 collective-permute-start.80
  538.3 8.5 %collective-permute-start.87 = (f32[4,128,64]{1,2,0:T(8,128)S(1)}, f32[4,128,64]{1,2,0:T(8,128)S(1)}, u32[]{:S(2)}, u32[]{:S(2)}) collective-permute-start(f32[4,128,64]{1,2,0:T(8,128)S(1)} %add.384), channel_id=1, source_target_pairs={{2,0},{3,1},{0,2},{1,3},{6,4},{7,5},{4,6},{5,7},{10,8},{11,9},{8,1... | collective-permute-start | bytes 393224 | tf_op jit(solution)/shard_map/ppermute | solution.py:39
  538.9 8.0 %collective-permute-start.86 = (f32[4,128,64]{1,2,0:T(8,128)S(1)}, f32[4,128,64]{1,2,0:T(8,128)S(1)}, u32[]{:S(2)}, u32[]{:S(2)}) collective-permute-start(f32[4,128,64]{1,2,0:T(8,128)S(1)} %add.384), channel_id=1, source_target_pairs={{1,0},{2,1},{3,2},{0,3},{5,4},{6,5},{7,6},{4,7},{9,8},{10,9},{11,1... | collective-permute-start | bytes 393224 | tf_op jit(solution)/shard_map/ppermute | solution.py:39
  539.9 7.2 %collective-permute-start.84 = (f32[4,128,32]{1,2,0:T(8,128)S(1)}, f32[4,128,32]{1,2,0:T(8,128)S(1)}, u32[]{:S(2)}, u32[]{:S(2)}) collective-permute-start(f32[4,128,32]{1,2,0:T(8,128)S(1)} %add.379), channel_id=1, source_target_pairs={{3,0},{0,1},{1,2},{2,3},{7,4},{4,5},{5,6},{6,7},{11,8},{8,9},{9,10... | collective-permute-start | bytes 196616 | tf_op jit(solution)/shard_map/ppermute | solution.py:39
  541.1 6.4 %collective-permute-start.83 = (f32[4,128,32]{1,2,0:T(8,128)S(1)}, f32[4,128,32]{1,2,0:T(8,128)S(1)}, u32[]{:S(2)}, u32[]{:S(2)}) collective-permute-start(f32[4,128,32]{1,2,0:T(8,128)S(1)} %add.379), channel_id=1, source_target_pairs={{2,0},{3,1},{0,2},{1,3},{6,4},{7,5},{4,6},{5,7},{10,8},{11,9},{8,1... | collective-permute-start | bytes 196616 | tf_op jit(solution)/shard_map/ppermute | solution.py:39
  543.5 4.7 collective-permute-start.82
  548.6 4.6 collective-permute-start.91
  548.7 4.3 collective-permute-start.90
  557.2 22.9 %collective-permute-start.95 = (f32[2,32]{1,0:T(2,128)S(1)}, f32[2,32]{1,0:T(2,128)S(1)}, u32[]{:S(2)}, u32[]{:S(2)}) collective-permute-start(f32[2,32]{1,0:T(2,128)S(1)} %add.389), channel_id=1, source_target_pairs={{96,0},{97,1},{98,2},{99,3},{100,4},{101,5},{102,6},{103,7},{104,8... | collective-permute-start | bytes 776 | tf_op jit(solution)/shard_map/ppermute | solution.py:39
  562.3 17.8 %collective-permute-start.94 = (f32[2,32]{1,0:T(2,128)S(1)}, f32[2,32]{1,0:T(2,128)S(1)}, u32[]{:S(2)}, u32[]{:S(2)}) collective-permute-start(f32[2,32]{1,0:T(2,128)S(1)} %add.389), channel_id=1, source_target_pairs={{64,0},{65,1},{66,2},{67,3},{68,4},{69,5},{70,6},{71,7},{72,8},{73... | collective-permute-start | bytes 776 | tf_op jit(solution)/shard_map/ppermute | solution.py:39
  571.2 11.2 %collective-permute-start.93 = (f32[2,32]{1,0:T(2,128)S(1)}, f32[2,32]{1,0:T(2,128)S(1)}, u32[]{:S(2)}, u32[]{:S(2)}) collective-permute-start(f32[2,32]{1,0:T(2,128)S(1)} %add.389), channel_id=1, source_target_pairs={{32,0},{33,1},{34,2},{35,3},{36,4},{37,5},{38,6},{39,7},{40,8},{41... | collective-permute-start | bytes 776 | tf_op jit(solution)/shard_map/ppermute | solution.py:39
  (133 other events, 1341.9 us)
